TPU v7x, 128 devices: a whole 4x4x4 slice. The times are simulated.
128 devices in a mesh: mech: 16 (over x, z), bin: 8 (over y, core).
Axes of the slice: x: 4, y: 4, z: 4, core: 2. Of those that a mesh axis runs over, the one named last changes fastest.
Arguments:
- face_coords: float32 [27, 262144], P(None, ('mech', 'bin')), may hold values from -1.03 to 1.03, as said below
- face_stiff: float32 [262144], P(('mech', 'bin')), may hold values from 1 to 10
- bin_order: int32 [128, 2048], P(('mech', 'bin')), may hold values from 0 to 2047, each once within a row
- slave_pos: float32 [3, 524288], P(None, ('mech', 'bin')), may hold values from -1.3 to 1.3, as said below
- slave_dest: int32 [524288, 1], P(('mech', 'bin')), may hold values from 0 to 127, as said below
- face_slot: int32 [524288], P(('mech', 'bin')), may hold values from 0 to 2047
- block_count: int32 [128, 32], P(('mech', 'bin')), may hold values from 64 to 128
- mirror_face: int32 [262144], P(('mech', 'bin')), may hold values from 0 to 2047
- mirror_node: int32 [262144], P(('mech', 'bin')), may hold values from 0 to 8
- mirror_dest: int32 [262144, 1], P(('mech', 'bin')), may hold values from 0 to 127, as said below
- mirror_slot: int32 [262144], P(('mech', 'bin')), may hold values from 0 to 2047
Outputs:
- slave_force: float32 [3, 524288], P(None, ('mech', 'bin'))
- face_force: float32 [27, 262144], P(None, ('mech', 'bin'))
Inputs may be any that keep to these rules, and one draw needn't show every extreme that they name: `face_coords`: node a = i + 3 j of every face lies within 0.03 of (i - 1, j - 1) in its first two components; its third component lies in -0.35 to 0.35. `slave_pos`: first two components lie in -1.3 to 1.3, the third in -0.6 to 0.6. `slave_dest`: among the rows of one device, no bin device is named by more than 64 rows, no element owner holds the named faces of more than 64 rows, and no bin device together with one owner by more than 64 // 8 rows; some bin device and some owner reach 64 from every device. `mirror_dest`: among the rows of one device, no partner device is named by more than 32 rows, no element owner holds the named faces of more than 32 rows, and no partner device together with one owner by more than 32 // 8 rows; some partner device and some owner reach 32 from every device. `bin_order`: each row is a permutation of 0 to 2047.
All inputs are finite; a program needn't handle non-finite values.
Results may differ from a plain program's by a relative error of at most 0.0003.
Values sent between devices are 32-bit elements; how exact they have to be, the bound alone decides.
No kernel may reach another device: no remote copies, remote signals or barrier semaphores. Data moves between devices by JAX's collectives and lax.ppermute only.
A program may use at most 64 MiB of HBM per device.

v0:
```python
import functools

import jax
import jax.numpy as jnp
from jax import lax
from jax.experimental import pallas as pl
from jax.experimental.pallas import tpu as pltpu
from jax.sharding import PartitionSpec as P

NEWTON = 5
CLIP_EDGE = 1.1
F32 = jnp.float32
BF16 = jnp.bfloat16
I32 = jnp.int32
LANES = 128
SB = 32
MB = 16
FT = 16
DEV = 128
NBIN = 8
SK = 64
MK = 32


def iota(shape, dim):
    return lax.broadcasted_iota(I32, shape, dim)


def dot_nt(a, b):
    return lax.dot_general(a, b, (((1,), (1,)), ((), ())), preferred_element_type=F32)


def row_gather(row, lane, shape):
    return jnp.take_along_axis(jnp.broadcast_to(row, shape), lane, axis=1)


def call(body, out_shape, scratch=(), in_specs=None, cost=0):
    kwargs = {} if in_specs is None else {"in_specs": in_specs}
    return pl.pallas_call(
        body,
        out_shape=out_shape,
        scratch_shapes=list(scratch),
        cost_estimate=pl.CostEstimate(flops=cost, bytes_accessed=cost // 100, transcendentals=0),
        **kwargs,
    )


VM = pl.BlockSpec(memory_space=pltpu.VMEM)
SM = pl.BlockSpec(memory_space=pltpu.SMEM)


def pack_body(
    count_ref, sdest_ref, sslot_ref, spos_ref, mdest_ref, mslot_ref, mface_ref, mnode_ref, coords_ref,
    send_ref, speer_ref, sk_ref, mpeer_ref, mk_ref,
    cell_ref, e_ref, b_ref, code_ref, cols_ref, hot_ref, val_ref, mval_ref, cnt_ref, pts_ref, rows_ref,
):
    def keys(dest, slot):
        owner = (dest & ~(NBIN - 1)) | (slot >> 8)
        return owner, dest & (NBIN - 1), (slot & 255) + 1

    owner, col, code = keys(sdest_ref[...], sslot_ref[...])
    e_ref[0:SB] = owner
    b_ref[0:SB] = col
    code_ref[0:SB] = code.astype(F32)
    speer_ref[...] = owner
    cell_ref[0:SB] = (owner * NBIN + col).astype(F32)
    owner, col, code = keys(mdest_ref[...], mslot_ref[...])
    e_ref[SB:SB + MB] = owner
    b_ref[SB:SB + MB] = col
    code_ref[SB:SB + MB] = code.astype(F32)
    mpeer_ref[...] = owner
    cell_ref[SB:SB + MB] = (owner * NBIN + col).astype(F32)
    cell_ref[SB + MB:] = jnp.zeros((LANES - SB - MB, LANES), F32)
    cols_ref[...] = cell_ref[...].T

    sub = iota((LANES, LANES), 0)
    lane_row = iota((1, LANES), 1)
    earlier = sub < iota((LANES, LANES), 1)
    sub8 = iota((NBIN, LANES), 0)
    sub16 = iota((16, LANES), 0)

    for r in range(SB + MB):
        hot = jnp.where(sub == e_ref[r:r + 1, :], 1.0, 0.0).astype(BF16)
        hot_ref[:, r * LANES:(r + 1) * LANES] = hot
        bins = jnp.where(sub16 == b_ref[r:r + 1, :], 1.0, 0.0).astype(BF16)
        cnt_ref[r] = dot_nt(bins, hot)[:NBIN]

    for first, last, cap, rows, vals, kout in (
        (0, SB, 8, SK, val_ref, sk_ref),
        (SB, SB + MB, 4, MK, mval_ref, mk_ref),
    ):
        seen = jnp.zeros((NBIN, LANES), F32)
        slot_iota = iota((rows, LANES), 0)
        for r in range(first, last):
            i = r - first
            peers = jnp.broadcast_to(e_ref[r:r + 1, :], (NBIN, LANES))
            before = jnp.where(
                sub8 == b_ref[r:r + 1, :], jnp.take_along_axis(seen, peers, axis=1), 0.0
            )
            same = cell_ref[r:r + 1, :] == cols_ref[:, r:r + 1]
            inside = jnp.where(same & earlier, 1.0, 0.0)
            rank = jnp.sum(inside, 0, keepdims=True) + jnp.sum(before, 0, keepdims=True)
            k = b_ref[r:r + 1, :] * cap + rank.astype(I32)
            if first == 0:
                k = jnp.where(lane_row < count_ref[0, i], k, -1)
            kout[i:i + 1, :] = k
            mine = slot_iota == k
            vals[0:rows, i * LANES:(i + 1) * LANES] = jnp.where(mine, float(i + 1), 0.0).astype(BF16)
            vals[rows:2 * rows, i * LANES:(i + 1) * LANES] = jnp.where(
                mine, lane_row.astype(F32), 0.0
            ).astype(BF16)
            seen = seen + cnt_ref[r]

    face = mface_ref[...]
    tile = face >> 7
    lane = face & 127
    node = mnode_ref[...]
    for c in range(3):
        point = jnp.zeros((MB, LANES), F32)
        for n in range(9):
            part = jnp.zeros((MB, LANES), F32)
            for t in range(FT):
                got = row_gather(
                    coords_ref[3 * n + c:3 * n + c + 1, t * LANES:(t + 1) * LANES], lane, (MB, LANES)
                )
                part = jnp.where(tile == t, got, part)
            point = jnp.where(node == n, part, point)
        pts_ref[c] = point

    sinv = dot_nt(val_ref[...], hot_ref[:, 0:SB * LANES])
    source = sinv[0:SK].astype(I32) - 1
    lane = sinv[SK:2 * SK].astype(I32)
    for c in range(4):
        out = jnp.zeros((SK, LANES), F32)
        for r in range(SB):
            if c < 3:
                row = spos_ref[c:c + 1, r * LANES:(r + 1) * LANES]
            else:
                row = code_ref[r:r + 1, :]
            out = jnp.where(source == r, row_gather(row, lane, (SK, LANES)), out)
        rows_ref[c * SK:(c + 1) * SK] = out
    minv = dot_nt(mval_ref[...], hot_ref[:, SB * LANES:])
    source = minv[0:MK].astype(I32) - 1
    lane = minv[MK:2 * MK].astype(I32)
    for c in range(4):
        out = jnp.zeros((MK, LANES), F32)
        for r in range(MB):
            if c < 3:
                row = pts_ref[c, r:r + 1, :]
            else:
                row = code_ref[SB + r:SB + r + 1, :]
            out = jnp.where(source == r, row_gather(row, lane, (MK, LANES)), out)
        rows_ref[4 * SK + c * MK:4 * SK + (c + 1) * MK] = out
    for i in range(3):
        send_ref[pl.ds(i, DEV, stride=3), :] = rows_ref[i * LANES:(i + 1) * LANES].T


def pack(count, sdest, sslot, spos, mdest, mslot, mface, mnode, coords):
    blocks = SB + MB
    return call(
        pack_body,
        (
            jax.ShapeDtypeStruct((3 * DEV, LANES), F32),
            jax.ShapeDtypeStruct((SB, LANES), I32),
            jax.ShapeDtypeStruct((SB, LANES), I32),
            jax.ShapeDtypeStruct((MB, LANES), I32),
            jax.ShapeDtypeStruct((MB, LANES), I32),
        ),
        [
            pltpu.VMEM((LANES, LANES), F32),
            pltpu.VMEM((blocks, LANES), I32),
            pltpu.VMEM((blocks, LANES), I32),
            pltpu.VMEM((blocks, LANES), F32),
            pltpu.VMEM((LANES, LANES), F32),
            pltpu.VMEM((LANES, blocks * LANES), BF16),
            pltpu.VMEM((2 * SK, SB * LANES), BF16),
            pltpu.VMEM((2 * MK, MB * LANES), BF16),
            pltpu.VMEM((blocks, NBIN, LANES), F32),
            pltpu.VMEM((3, MB, LANES), F32),
            pltpu.VMEM((3 * LANES, LANES), F32),
        ],
        in_specs=[SM] + [VM] * 8,
        cost=10**9,
    )(count, sdest, sslot, spos, mdest, mslot, mface, mnode, coords)


def order_body(coords_ref, stiff_ref, order_ref, mface_ref, table_ref, inv_ref, mhot_ref, hot_ref, val_ref, src_ref):
    src_ref[0:27] = coords_ref[...]
    src_ref[27:28] = stiff_ref[...]
    src_ref[28:32] = jnp.zeros((4, FT * LANES), F32)
    sub = iota((LANES, LANES), 0)
    sub16 = iota((FT, LANES), 0)
    lane_row = iota((1, LANES), 1).astype(F32)
    for m in range(FT):
        order = order_ref[m:m + 1, :]
        hi = order >> 7
        lo = order & 127
        lane = jnp.broadcast_to(lo, (32, LANES))
        out = jnp.zeros((32, LANES), F32)
        for t in range(FT):
            got = jnp.take_along_axis(src_ref[:, t * LANES:(t + 1) * LANES], lane, axis=1)
            out = jnp.where(hi == t, got, out)
        table_ref[:, m * LANES:(m + 1) * LANES] = out
        hot_ref[:, m * LANES:(m + 1) * LANES] = jnp.where(sub == lo, 1.0, 0.0).astype(BF16)
        mine = sub16 == hi
        val_ref[0:FT, m * LANES:(m + 1) * LANES] = jnp.where(mine, float(m), 0.0).astype(BF16)
        val_ref[FT:2 * FT, m * LANES:(m + 1) * LANES] = jnp.where(mine, lane_row, 0.0).astype(BF16)
    inv_ref[...] = dot_nt(val_ref[...], hot_ref[...]).astype(I32)
    big = iota((FT * LANES, LANES), 0)
    for r in range(MB):
        mhot_ref[:, r * LANES:(r + 1) * LANES] = jnp.where(
            big == mface_ref[r:r + 1, :], 1.0, 0.0
        ).astype(BF16)


def order_faces(coords, stiff, order, mface):
    faces = FT * LANES
    return call(
        order_body,
        (
            jax.ShapeDtypeStruct((32, faces), F32),
            jax.ShapeDtypeStruct((2 * FT, LANES), I32),
            jax.ShapeDtypeStruct((faces, MB * LANES), BF16),
        ),
        [
            pltpu.VMEM((LANES, faces), BF16),
            pltpu.VMEM((2 * FT, faces), BF16),
            pltpu.VMEM((32, faces), F32),
        ],
        cost=10**9,
    )(coords, stiff, order, mface)


def quadratic(low, mid, high):
    return mid, 0.5 * (high - low), 0.5 * (high + low) - mid


def project(point, nodes, stiff):
    coef = []
    for c in range(3):
        by_j = [quadratic(nodes[3 * j][c], nodes[3 * j + 1][c], nodes[3 * j + 2][c]) for j in range(3)]
        coef.append([quadratic(by_j[0][p], by_j[1][p], by_j[2][p]) for p in range(3)])

    def surface(u, v):
        u2 = u + u
        v2 = v + v
        x, tu, tv = [], [], []
        for c in range(3):
            k = coef[c]
            h = [k[0][q] + u * (k[1][q] + u * k[2][q]) for q in range(3)]
            d = [k[1][q] + u2 * k[2][q] for q in range(3)]
            x.append(h[0] + v * (h[1] + v * h[2]))
            tu.append(d[0] + v * (d[1] + v * d[2]))
            tv.append(h[1] + v2 * h[2])
        return x, tu, tv

    def inner(a, b):
        return a[0] * b[0] + a[1] * b[1] + a[2] * b[2]

    u = v = jnp.zeros_like(point[0])
    for step in range(NEWTON):
        if step == 0:
            x = [coef[c][0][0] for c in range(3)]
            tu = [coef[c][1][0] for c in range(3)]
            tv = [coef[c][0][1] for c in range(3)]
        else:
            x, tu, tv = surface(u, v)
        o = [point[c] - x[c] for c in range(3)]
        a_uu, a_uv, a_vv = inner(tu, tu), inner(tu, tv), inner(tv, tv)
        b_u, b_v = inner(tu, o), inner(tv, o)
        scale = 1.0 / (a_uu * a_vv - a_uv * a_uv)
        du = (a_vv * b_u - a_uv * b_v) * scale
        dv = (a_uu * b_v - a_uv * b_u) * scale
        u = jnp.clip(u + du, -CLIP_EDGE, CLIP_EDGE)
        v = jnp.clip(v + dv, -CLIP_EDGE, CLIP_EDGE)
    x, tu, tv = surface(u, v)
    n = [
        tu[1] * tv[2] - tu[2] * tv[1],
        tu[2] * tv[0] - tu[0] * tv[2],
        tu[0] * tv[1] - tu[1] * tv[0],
    ]
    unit = 1.0 / jnp.sqrt(inner(n, n))
    gap = inner([point[c] - x[c] for c in range(3)], n) * unit
    size = 0.5 * stiff * jnp.maximum(-gap, 0.0) * unit
    return u, v, [size * n[c] for c in range(3)]


def force_body(recv_ref, table_ref, back_ref, uv_ref, force_ref, index_ref, rows_ref):
    for i in range(3):
        rows_ref[i * LANES:(i + 1) * LANES] = recv_ref[pl.ds(i, DEV, stride=3), :].T
    shape = (8, LANES)
    upper = iota(shape, 0) < 4
    force_ref[3 * SK + 3 * MK:] = jnp.zeros((LANES - 32, LANES), F32)
    for g in range(12):
        if g < 8:
            at = [c * SK + g * 8 for c in range(4)]
            out = [c * SK + g * 8 for c in range(3)]
        else:
            at = [4 * SK + c * MK + (g - 8) * 8 for c in range(4)]
            out = [3 * SK + c * MK + (g - 8) * 8 for c in range(3)]
        point = [rows_ref[at[c]:at[c] + 8, :] for c in range(3)]
        code = rows_ref[at[3]:at[3] + 8, :].astype(I32)
        index = jnp.maximum(code - 1, 0)
        lane = index & 127
        high = index >= LANES

        def entry(row, half):
            def tile(t):
                return jnp.broadcast_to(table_ref[row:row + 1, t * LANES:(t + 1) * LANES], shape)

            if g < 8:
                return tile(2 * g + half)
            first = 4 * (g - 8)
            return jnp.where(upper, tile(first + half), tile(first + 2 + half))

        def pick(row):
            got = [jnp.take_along_axis(entry(row, half), lane, axis=1) for half in range(2)]
            return jnp.where(high, got[1], got[0])

        nodes = [[pick(3 * a + c) for c in range(3)] for a in range(9)]
        stiff = jnp.where(code > 0, pick(27), 0.0)
        u, v, force = project(point, nodes, stiff)
        uv_ref[g * 8:g * 8 + 8] = u
        uv_ref[96 + g * 8:96 + g * 8 + 8] = v
        index_ref[g * 8:g * 8 + 8] = index
        for c in range(3):
            force_ref[out[c]:out[c] + 8] = force[c]
    for i in range(3):
        back_ref[pl.ds(i, DEV, stride=3), :] = force_ref[i * LANES:(i + 1) * LANES].T


def forces(recv, table):
    return call(
        force_body,
        (
            jax.ShapeDtypeStruct((3 * DEV, LANES), F32),
            jax.ShapeDtypeStruct((192, LANES), F32),
            jax.ShapeDtypeStruct((3 * LANES, LANES), F32),
            jax.ShapeDtypeStruct((96, LANES), I32),
        ),
        [pltpu.VMEM((3 * LANES, LANES), F32)],
        cost=10**9,
    )(recv, table)


def split(x):
    high = x.astype(BF16)
    return high, (x - high.astype(F32)).astype(BF16)


def react_body(uv_ref, force_ref, index_ref, inv_ref, out_ref, part_ref, lhs_ref, hot_ref, sum_ref):
    part_ref[27 * 8:] = jnp.zeros((40, LANES), F32)
    sub = iota((2 * LANES, LANES), 0)

    def fill(g, first, count, at):
        for k in range(count):
            rows = part_ref[pl.ds(first + k, 32, stride=8), :]
            high, low = split(rows)
            lhs_ref[0:32, (at + k) * LANES:(at + k + 1) * LANES] = high
            lhs_ref[32:64, (at + k) * LANES:(at + k + 1) * LANES] = low
            row = g * 8 + first + k
            hot_ref[:, (at + k) * LANES:(at + k + 1) * LANES] = jnp.where(
                sub == index_ref[row:row + 1, :], 1.0, 0.0
            ).astype(BF16)

    def reactions(g):
        u = uv_ref[g * 8:g * 8 + 8]
        v = uv_ref[96 + g * 8:96 + g * 8 + 8]
        lu = (u * (u - 1.0) * 0.5, 1.0 - u * u, u * (u + 1.0) * 0.5)
        lv = (v * (v - 1.0) * 0.5, 1.0 - v * v, v * (v + 1.0) * 0.5)
        for c in range(3):
            row = c * SK + g * 8 if g < 8 else 3 * SK + c * MK + (g - 8) * 8
            f = -force_ref[row:row + 8]
            for j in range(3):
                fj = f * lv[j]
                for i in range(3):
                    a = 3 * (i + 3 * j) + c
                    part_ref[a * 8:a * 8 + 8] = lu[i] * fj

    for b in range(NBIN):
        reactions(b)
        fill(b, 0, 8, 0)
        reactions(8 + b // 2)
        fill(8 + b // 2, 4 * (b % 2), 4, 8)
        both = dot_nt(lhs_ref[...], hot_ref[...])
        sum_ref[:, b * 256:(b + 1) * 256] = both[0:32] + both[32:64]

    for m in range(FT):
        hi = inv_ref[m:m + 1, :]
        lane = jnp.broadcast_to(inv_ref[FT + m:FT + m + 1, :], (32, LANES))
        out = jnp.zeros((32, LANES), F32)
        for t in range(FT):
            got = jnp.take_along_axis(sum_ref[:, t * LANES:(t + 1) * LANES], lane, axis=1)
            out = jnp.where(hi == t, got, out)
        out_ref[:, m * LANES:(m + 1) * LANES] = out


def react(uv, force, index, inv):
    return call(
        react_body,
        jax.ShapeDtypeStruct((32, FT * LANES), F32),
        [
            pltpu.VMEM((256, LANES), F32),
            pltpu.VMEM((64, 12 * LANES), BF16),
            pltpu.VMEM((256, 12 * LANES), BF16),
            pltpu.VMEM((32, FT * LANES), F32),
        ],
        cost=10**9,
    )(uv, force, index, inv)


def finish_body(
    back_ref, speer_ref, sk_ref, mpeer_ref, mk_ref, mnode_ref, mhot_ref, part_ref,
    slave_ref, face_ref, rows_ref, own_ref, lhs_ref,
):
    for i in range(3):
        rows_ref[i * LANES:(i + 1) * LANES] = back_ref[pl.ds(i, DEV, stride=3), :].T
    peer = mpeer_ref[...]
    slot = mk_ref[...]
    for c in range(3):
        out = jnp.zeros((MB, LANES), F32)
        for k in range(MK):
            row = 3 * SK + c * MK + k
            out = jnp.where(slot == k, row_gather(rows_ref[row:row + 1, :], peer, (MB, LANES)), out)
        own_ref[c] = out
    sub = iota((32, LANES), 0)
    comp = sub % 3
    node = sub // 3
    for r in range(MB):
        f = jnp.where(comp == 0, own_ref[0, r:r + 1, :], own_ref[1, r:r + 1, :])
        f = jnp.where(comp == 2, own_ref[2, r:r + 1, :], f)
        f = jnp.where(node == mnode_ref[r:r + 1, :], f, 0.0)
        high, low = split(f)
        lhs_ref[0:32, r * LANES:(r + 1) * LANES] = high
        lhs_ref[32:64, r * LANES:(r + 1) * LANES] = low
    both = dot_nt(lhs_ref[...], mhot_ref[...])
    face_ref[...] = (part_ref[...] + both[0:32] + both[32:64])[0:27]

    peer = speer_ref[...]
    slot = sk_ref[...]
    for c in range(3):
        out = jnp.zeros((SB, LANES), F32)
        for k in range(SK):
            row = c * SK + k
            out = jnp.where(slot == k, row_gather(rows_ref[row:row + 1, :], peer, (SB, LANES)), out)
        for r in range(SB):
            slave_ref[c:c + 1, r * LANES:(r + 1) * LANES] = out[r:r + 1, :]


def finish(back, speer, sk, mpeer, mk, mnode, mhot, part):
    return call(
        finish_body,
        (
            jax.ShapeDtypeStruct((3, SB * LANES), F32),
            jax.ShapeDtypeStruct((27, FT * LANES), F32),
        ),
        [
            pltpu.VMEM((3 * LANES, LANES), F32),
            pltpu.VMEM((3, MB, LANES), F32),
            pltpu.VMEM((64, MB * LANES), BF16),
        ],
        cost=10**9,
    )(back, speer, sk, mpeer, mk, mnode, mhot, part)


def exchange(x):
    x = x.reshape(DEV, 1, 3 * LANES)
    x = lax.all_to_all(x, ("mech", "bin"), split_axis=0, concat_axis=0, tiled=True)
    return x.reshape(3 * DEV, LANES)


def shards(
    face_coords, face_stiff, bin_order, slave_pos, slave_dest, face_slot, block_count,
    mirror_face, mirror_node, mirror_dest, mirror_slot,
):
    mface = mirror_face.reshape(MB, LANES)
    mnode = mirror_node.reshape(MB, LANES)
    send, speer, sk, mpeer, mk = pack(
        block_count,
        slave_dest.reshape(SB, LANES),
        face_slot.reshape(SB, LANES),
        slave_pos,
        mirror_dest.reshape(MB, LANES),
        mirror_slot.reshape(MB, LANES),
        mface,
        mnode,
        face_coords,
    )
    recv = exchange(send)
    table, inv, mhot = order_faces(
        face_coords, face_stiff.reshape(1, FT * LANES), bin_order.reshape(FT, LANES), mface
    )
    back, uv, force, index = forces(recv, table)
    returned = exchange(back)
    part = react(uv, force, index, inv)
    return finish(returned, speer, sk, mpeer, mk, mnode, mhot, part)


def solution(mesh):
    axes = ("mech", "bin")
    return jax.shard_map(
        shards,
        mesh=mesh,
        in_specs=(
            P(None, axes), P(axes), P(axes, None), P(None, axes), P(axes, None), P(axes),
            P(axes, None), P(axes), P(axes), P(axes, None), P(axes),
        ),
        out_specs=(P(None, axes), P(None, axes)),
        check_vma=False,
    )
```

profile of v0, /device:TPU:1, one launch (start us, length us, event | category | flops | bytes accessed | tf_op | source)
XLA Modules:
  0.0 64.4 jit_solution(4973563898817594616)
XLA Ops:
  0.6 9.4 %shard_map.122 = (f32[384,128]{1,0:T(8,128)}, s32[32,128]{1,0:T(8,128)}, s32[32,128]{1,0:T(8,128)}, s32[16,128]{1,0:T(8,128)}, s32[16,128]{1,0:T(8,128)}) custom-call(s32[1,32]{1,0:T(1,128)} %count_ref.1, s32[32,128]{1,0:T(8,128)} %bitcast.18, s32[32,128]{1,0:T(8,128)} %bitcast.19, f32[3,4096]{1,0:T(4,128)} %spos_ref.1, s32[16,128]{1,0:T(8,128)} %bitcast.20, ...), custom_call_target="tpu_custom_call" | custom-call | flops 1000000000 | bytes 10000000 | tf_op jit(solution)/shard_map/pallas_call | solution.py:160
  10.0 11.5 %all-to-all-start = ((f32[128,1,384]{2,1,0:T(1,128)}), f32[128,1,384]{2,1,0:T(1,128)S(1)}, u32[]{:S(2)}, u32[]{:S(2)}) async-start(f32[128,1,384]{2,1,0:T(1,128)} %bitcast.14), calls=%async_computation | async-start | bytes 393216 | tf_op jit(solution)/shard_map/all_to_all | solution.py:468
  21.5 10.5 %shard_map.123 = (f32[32,2048]{1,0:T(8,128)}, s32[32,128]{1,0:T(8,128)}, bf16[2048,2048]{1,0:T(8,128)(2,1)}) custom-call(f32[27,2048]{1,0:T(8,128)} %coords_ref.3, f32[1,2048]{1,0:T(1,128)} %bitcast.24, s32[16,128]{1,0:T(8,128)} %bitcast.25, s32[16,128]{1,0:T(8,128)} %bitcast.23), custom_call_target="tpu_custom_call" | custom-call | flops 1000000000 | bytes 10000000 | tf_op jit(solution)/shard_map/pallas_call | solution.py:218
  32.0 0.0 all-to-all-done
  32.0 0.0 copy-start.1
  32.0 0.7 %copy-done.1 = f32[128,1,384]{2,1,0:T(1,128)} copy-done((f32[128,1,384]{2,1,0:T(1,128)}, f32[128,1,384]{2,1,0:T(1,128)S(1)}, u32[]{:S(2)}) %copy-start.1) | copy-done | bytes 196632
  32.7 3.6 %shard_map.124 = (f32[384,128]{1,0:T(8,128)}, f32[192,128]{1,0:T(8,128)}, f32[384,128]{1,0:T(8,128)}, s32[96,128]{1,0:T(8,128)}) custom-call(f32[384,128]{1,0:T(8,128)} %bitcast.13, f32[32,2048]{1,0:T(8,128)} %get-tuple-element.15.table_ref), custom_call_target="tpu_custom_call" | custom-call | flops 1000000000 | bytes 10000000 | tf_op jit(solution)/shard_map/pallas_call | solution.py:333
  36.3 9.8 %all-to-all-start.1 = ((f32[128,1,384]{2,1,0:T(1,128)}), f32[128,1,384]{2,1,0:T(1,128)S(1)}, u32[]{:S(2)}, u32[]{:S(2)}) async-start(f32[128,1,384]{2,1,0:T(1,128)} %bitcast.15), calls=%async_computation.1 | async-start | bytes 393216 | tf_op jit(solution)/shard_map/all_to_all | solution.py:468
  46.1 5.6 %shard_map.125.part_ref = f32[32,2048]{1,0:T(8,128)} custom-call(f32[192,128]{1,0:T(8,128)} %get-tuple-element.22.uv_ref, f32[384,128]{1,0:T(8,128)} %get-tuple-element.23.force_ref, s32[96,128]{1,0:T(8,128)} %get-tuple-element.24.index_ref, s32[32,128]{1,0:T(8,128)} %get-tuple-element.25.inv_ref), custom_call_target="tpu_custom_call" | custom-call | flops 1000000000 | bytes 10000000 | tf_op jit(solution)/shard_map/pallas_call | solution.py:399
  51.7 4.8 %all-to-all-done.1 = f32[128,1,384]{2,1,0:T(1,128)S(1)} async-done(((f32[128,1,384]{2,1,0:T(1,128)}), f32[128,1,384]{2,1,0:T(1,128)S(1)}, u32[]{:S(2)}, u32[]{:S(2)}) %all-to-all-start.1) | async-done | bytes 196640 | tf_op jit(solution)/shard_map/all_to_all | solution.py:468
  56.4 0.0 copy-start
  56.4 0.7 %copy-done = f32[128,1,384]{2,1,0:T(1,128)} copy-done((f32[128,1,384]{2,1,0:T(1,128)}, f32[128,1,384]{2,1,0:T(1,128)S(1)}, u32[]{:S(2)}) %copy-start) | copy-done | bytes 196632
  57.1 7.3 %shard_map.126 = (f32[3,4096]{1,0:T(4,128)}, f32[27,2048]{1,0:T(8,128)}) custom-call(f32[384,128]{1,0:T(8,128)} %bitcast.12, s32[32,128]{1,0:T(8,128)} %get-tuple-element.17.speer_ref, s32[32,128]{1,0:T(8,128)} %get-tuple-element.18.sk_ref, s32[16,128]{1,0:T(8,128)} %get-tuple-element.19.mpeer_ref, s32[16,128]{1,0:T(8,128)} %get-tuple-element.20.mk_ref, ...), custom_call_target="tpu_custom_call" | custom-call | flops 1000000000 | bytes 10000000 | tf_op jit(solution)/shard_map/pallas_call | solution.py:451
Async XLA Ops:
  10.0 22.0 %all-to-all-start = ((f32[128,1,384]{2,1,0:T(1,128)}), f32[128,1,384]{2,1,0:T(1,128)S(1)}, u32[]{:S(2)}, u32[]{:S(2)}) async-start(f32[128,1,384]{2,1,0:T(1,128)} %bitcast.14), calls=%async_computation | async-start | bytes 393216 | tf_op jit(solution)/shard_map/all_to_all | solution.py:468
  32.0 0.7 %copy-start.1 = (f32[128,1,384]{2,1,0:T(1,128)}, f32[128,1,384]{2,1,0:T(1,128)S(1)}, u32[]{:S(2)}) copy-start(f32[128,1,384]{2,1,0:T(1,128)S(1)} %all-to-all-done) | copy-start | bytes 589828
  36.3 20.2 %all-to-all-start.1 = ((f32[128,1,384]{2,1,0:T(1,128)}), f32[128,1,384]{2,1,0:T(1,128)S(1)}, u32[]{:S(2)}, u32[]{:S(2)}) async-start(f32[128,1,384]{2,1,0:T(1,128)} %bitcast.15), calls=%async_computation.1 | async-start | bytes 393216 | tf_op jit(solution)/shard_map/all_to_all | solution.py:468
  56.4 0.7 %copy-start = (f32[128,1,384]{2,1,0:T(1,128)}, f32[128,1,384]{2,1,0:T(1,128)S(1)}, u32[]{:S(2)}) copy-start(f32[128,1,384]{2,1,0:T(1,128)S(1)} %all-to-all-done.1) | copy-start | bytes 589828
where the time goes:
time: 64.7 us; the launch traced here: 64.4 us
  Pallas kernels  36.4 us (56%)
  starting transfers between devices  21.3 us (33%)
  waiting for transfers between devices  4.75 us (7%)
  local copies, waits for them, and re-layouts  1.37 us (2%)
  between operations  0.65 us (1%)
    all_to_all x2, starting transfers between devices, exchange(): lax.all_to_all(x, ('mech', 'bin'), split_axis=0, concat_axis=0, tiled=True)  21.3 us
    pallas_call x1, Pallas kernels, order_faces(): call(order_body, (jax.ShapeDtypeStruct((32, faces), F32), jax.ShapeDtypeS...  10.5 us
    pallas_call x1, Pallas kernels, pack(): call(pack_body, (jax.ShapeDtypeStruct((3 * DEV, LANES), F32), jax.ShapeDt...  9.37 us
    pallas_call x1, Pallas kernels, finish(): call(finish_body, (jax.ShapeDtypeStruct((3, SB * LANES), F32), jax.ShapeD...  7.29 us
    pallas_call x1, Pallas kernels, react(): call(react_body, jax.ShapeDtypeStruct((32, FT * LANES), F32), [pltpu.VMEM...  5.62 us
    all_to_all x2, waiting for transfers between devices, exchange(): lax.all_to_all(x, ('mech', 'bin'), split_axis=0, concat_axis=0, tiled=True)  4.75 us
    pallas_call x1, Pallas kernels, forces(): call(force_body, (jax.ShapeDtypeStruct((3 * DEV, LANES), F32), jax.ShapeD...  3.55 us
    unnamed x4, local copies, waits for them, and re-layouts  1.37 us
  transfers between devices with their start and end apart: 2, of which 1 were waited for; matrix products, arithmetic and copies ran while one was open for 0% of the time, Pallas kernels for 25%

commit v1 on v0

v1 whole, which is shorter than its diff:
```python
import functools

import jax
import jax.numpy as jnp
from jax import lax
from jax.experimental import pallas as pl
from jax.experimental.pallas import tpu as pltpu
from jax.sharding import PartitionSpec as P

NEWTON = 5
CLIP_EDGE = 1.1
VMEM_BYTES = 16 * 2**20
F32 = jnp.float32
BF16 = jnp.bfloat16
I32 = jnp.int32
I16 = jnp.int16
LANES = 128
SB = 32
MB = 16
FT = 16
DEV = 128
NBIN = 8
SK = 64
MK = 32


def iota(shape, dim):
    return lax.broadcasted_iota(I32, shape, dim)


def dot_nt(a, b):
    return lax.dot_general(a, b, (((1,), (1,)), ((), ())), preferred_element_type=F32)


def wide16(row, rows):
    narrow = jnp.broadcast_to(row, (16, LANES)).astype(I16)
    return jnp.concatenate([narrow] * (rows // 16), 0) if rows > 16 else narrow


def slot_rows(rows):
    return iota((rows, LANES), 0).astype(I16)


def pick_bf16(rows16, row):
    hit = rows16 == wide16(row, rows16.shape[0])
    return jnp.where(hit, jnp.ones(rows16.shape, BF16), jnp.zeros(rows16.shape, BF16))


def one_hot(rows, row):
    return pick_bf16(slot_rows(rows), row)


def row_gather(row, lane, shape):
    return jnp.take_along_axis(jnp.broadcast_to(row, shape), lane, axis=1)


def call(body, out_shape, scratch=(), in_specs=None, cost=0):
    kwargs = {} if in_specs is None else {"in_specs": in_specs}
    return pl.pallas_call(
        body,
        out_shape=out_shape,
        scratch_shapes=list(scratch),
        compiler_params=pltpu.CompilerParams(vmem_limit_bytes=VMEM_BYTES),
        cost_estimate=pl.CostEstimate(flops=cost, bytes_accessed=cost // 100, transcendentals=0),
        **kwargs,
    )


VM = pl.BlockSpec(memory_space=pltpu.VMEM)
SM = pl.BlockSpec(memory_space=pltpu.SMEM)


def pack_body(
    count_ref, sdest_ref, sslot_ref, spos_ref, mdest_ref, mslot_ref, mface_ref, mnode_ref, coords_ref,
    send_ref, speer_ref, sk_ref, mpeer_ref, mk_ref,
    cell_ref, e_ref, b_ref, code_ref, turn_ref, cols_ref, cnt_ref, pts_ref, rows_ref,
):
    def keys(dest, slot):
        owner = (dest & ~(NBIN - 1)) | (slot >> 8)
        return owner, dest & (NBIN - 1), (slot & 255) + 1

    half = LANES // 2
    for first, rows, dest_ref, slot_ref, peer_ref in (
        (0, SB, sdest_ref, sslot_ref, speer_ref),
        (SB, MB, mdest_ref, mslot_ref, mpeer_ref),
    ):
        owner, col, code = keys(dest_ref[...], slot_ref[...])
        e_ref[first:first + rows] = owner
        b_ref[first:first + rows] = col
        code_ref[first:first + rows] = code.astype(F32)
        peer_ref[...] = owner
        cell = (owner * NBIN + col).astype(F32)
        cell_ref[first:first + rows] = cell
        turn_ref[first:first + rows] = cell
        turn_ref[half + first:half + first + rows] = pltpu.roll(cell, half, axis=1)
    for first in (SB + MB, half + SB + MB):
        turn_ref[first:first + half - SB - MB] = jnp.zeros((half - SB - MB, LANES), F32)
    cols_ref[...] = turn_ref[...].T

    lane_row = iota((1, LANES), 1)
    lane8 = iota((NBIN, LANES), 1)
    earlier = iota((half, LANES), 0) < (iota((half, LANES), 1) & (half - 1))
    sub8 = iota((NBIN, LANES), 0)
    upper = lane8 >= half
    row16 = iota((16, LANES), 0)
    bin_rows = jnp.where((row16 < 8) | (iota((16, LANES), 1) < half), row16 & 7, -1).astype(I16)
    lanes_bf = iota((64, LANES), 1).astype(F32).astype(BF16)

    for r in range(SB + MB):
        bins = pick_bf16(bin_rows, b_ref[r:r + 1, :])
        cnt_ref[r] = dot_nt(bins, one_hot(LANES, e_ref[r:r + 1, :]))

    def slots(first, last, cap, rows, kout):
        seen = jnp.zeros((NBIN, LANES), F32)
        inverse = jnp.zeros((2 * rows, LANES), F32)
        for group in range(first, last, 4):
            left, right = [], []
            for r in range(group, group + 4):
                i = r - first
                peers = jnp.broadcast_to(e_ref[r:r + 1, :], (NBIN, LANES))
                column = jnp.where(upper, half + r, r)
                before = jnp.take_along_axis(seen, peers, axis=1) + jnp.where(
                    upper, jnp.take_along_axis(cnt_ref[r, 8:16], peers, axis=1), 0.0
                )
                before = jnp.where(sub8 == b_ref[r:r + 1, :], before, 0.0)
                for m in range(half // 8):
                    col = jnp.take_along_axis(cols_ref[8 * m:8 * m + 8], column, axis=1)
                    same = (cell_ref[r:r + 1, :] == col) & earlier[8 * m:8 * m + 8]
                    before = before + jnp.where(same, 1.0, 0.0)
                rank = jnp.sum(before, 0, keepdims=True)
                k = b_ref[r:r + 1, :] * cap + rank.astype(I32)
                if first == 0:
                    k = jnp.where(lane_row < count_ref[0, i], k, -1)
                kout[i:i + 1, :] = k
                mine = slot_rows(rows) == wide16(k, rows)
                left.append(jnp.concatenate([
                    jnp.where(mine, jnp.full((rows, LANES), i + 1, BF16), jnp.zeros((rows, LANES), BF16)),
                    jnp.where(mine, lanes_bf[:rows], jnp.zeros((rows, LANES), BF16)),
                ], 0))
                right.append(one_hot(LANES, e_ref[r:r + 1, :]))
                seen = seen + cnt_ref[r, 0:8]
            inverse = inverse + dot_nt(jnp.concatenate(left, 1), jnp.concatenate(right, 1))
        return inverse

    sinv = slots(0, SB, 8, SK, sk_ref)
    minv = slots(SB, SB + MB, 4, MK, mk_ref)

    for m in range(MB // 8):
        face = mface_ref[8 * m:8 * m + 8]
        tile = face >> 7
        lane = face & 127
        node = mnode_ref[8 * m:8 * m + 8]
        at_tile = [tile == t for t in range(FT)]
        for c in range(3):
            point = jnp.zeros((8, LANES), F32)
            for n in range(9):
                part = jnp.zeros((8, LANES), F32)
                for t in range(FT):
                    got = row_gather(
                        coords_ref[3 * n + c:3 * n + c + 1, t * LANES:(t + 1) * LANES], lane, (8, LANES)
                    )
                    part = jnp.where(at_tile[t], got, part)
                point = jnp.where(node == n, part, point)
            pts_ref[c, 8 * m:8 * m + 8] = point

    for blocks, rows, inverse, base in ((SB, SK, sinv, 0), (MB, MK, minv, 4 * SK)):
        for m in range(rows // 8):
            source = inverse[8 * m:8 * m + 8].astype(I32) - 1
            lane = inverse[rows + 8 * m:rows + 8 * m + 8].astype(I32)
            at_block = [source == r for r in range(blocks)]
            for c in range(4):
                out = jnp.zeros((8, LANES), F32)
                for r in range(blocks):
                    if c == 3:
                        first = 0 if base == 0 else SB
                        row = code_ref[first + r:first + r + 1, :]
                    elif base == 0:
                        row = spos_ref[c:c + 1, r * LANES:(r + 1) * LANES]
                    else:
                        row = pts_ref[c, r:r + 1, :]
                    out = jnp.where(at_block[r], row_gather(row, lane, (8, LANES)), out)
                at = base + c * rows + 8 * m
                rows_ref[at:at + 8] = out
    for i in range(3):
        send_ref[pl.ds(i, DEV, stride=3), :] = rows_ref[i * LANES:(i + 1) * LANES].T


def pack(count, sdest, sslot, spos, mdest, mslot, mface, mnode, coords):
    blocks = SB + MB
    return call(
        pack_body,
        (
            jax.ShapeDtypeStruct((3 * DEV, LANES), F32),
            jax.ShapeDtypeStruct((SB, LANES), I32),
            jax.ShapeDtypeStruct((SB, LANES), I32),
            jax.ShapeDtypeStruct((MB, LANES), I32),
            jax.ShapeDtypeStruct((MB, LANES), I32),
        ),
        [
            pltpu.VMEM((blocks, LANES), F32),
            pltpu.VMEM((blocks, LANES), I32),
            pltpu.VMEM((blocks, LANES), I32),
            pltpu.VMEM((blocks, LANES), F32),
            pltpu.VMEM((LANES, LANES), F32),
            pltpu.VMEM((LANES, LANES), F32),
            pltpu.VMEM((blocks, 16, LANES), F32),
            pltpu.VMEM((3, MB, LANES), F32),
            pltpu.VMEM((3 * LANES, LANES), F32),
        ],
        in_specs=[SM] + [VM] * 8,
        cost=10**9,
    )(count, sdest, sslot, spos, mdest, mslot, mface, mnode, coords)


def order_body(coords_ref, stiff_ref, order_ref, table_ref, inv_ref, src_ref):
    src_ref[0:27] = coords_ref[...]
    src_ref[27:28] = stiff_ref[...]
    src_ref[28:32] = jnp.zeros((4, FT * LANES), F32)
    lanes_bf = iota((FT, LANES), 1).astype(F32).astype(BF16)
    zero = jnp.zeros((FT, LANES), BF16)
    inverse = jnp.zeros((2 * FT, LANES), F32)
    left, right = [], []
    for m in range(FT):
        order = order_ref[m:m + 1, :]
        hi = order >> 7
        lo = order & 127
        lane = jnp.broadcast_to(lo, (8, LANES))
        tile = jnp.broadcast_to(hi, (8, LANES))
        at_tile = [tile == t for t in range(FT)]
        for g in range(4):
            out = jnp.zeros((8, LANES), F32)
            for t in range(FT):
                got = jnp.take_along_axis(
                    src_ref[8 * g:8 * g + 8, t * LANES:(t + 1) * LANES], lane, axis=1
                )
                out = jnp.where(at_tile[t], got, out)
            table_ref[8 * g:8 * g + 8, m * LANES:(m + 1) * LANES] = out
        mine = slot_rows(FT) == wide16(hi, FT)
        left.append(jnp.concatenate([
            jnp.where(mine, jnp.full((FT, LANES), m, BF16), zero), jnp.where(mine, lanes_bf, zero)
        ], 0))
        right.append(one_hot(LANES, lo))
        if m % 4 == 3:
            inverse = inverse + dot_nt(jnp.concatenate(left, 1), jnp.concatenate(right, 1))
            left, right = [], []
    inv_ref[...] = inverse.astype(I32)


def order_faces(coords, stiff, order):
    faces = FT * LANES
    return call(
        order_body,
        (
            jax.ShapeDtypeStruct((32, faces), F32),
            jax.ShapeDtypeStruct((2 * FT, LANES), I32),
        ),
        [pltpu.VMEM((32, faces), F32)],
        cost=10**9,
    )(coords, stiff, order)


def quadratic(low, mid, high):
    return mid, 0.5 * (high - low), 0.5 * (high + low) - mid


def project(point, nodes, stiff):
    coef = []
    for c in range(3):
        by_j = [quadratic(nodes[3 * j][c], nodes[3 * j + 1][c], nodes[3 * j + 2][c]) for j in range(3)]
        coef.append([quadratic(by_j[0][p], by_j[1][p], by_j[2][p]) for p in range(3)])

    def surface(u, v):
        u2 = u + u
        v2 = v + v
        x, tu, tv = [], [], []
        for c in range(3):
            k = coef[c]
            h = [k[0][q] + u * (k[1][q] + u * k[2][q]) for q in range(3)]
            d = [k[1][q] + u2 * k[2][q] for q in range(3)]
            x.append(h[0] + v * (h[1] + v * h[2]))
            tu.append(d[0] + v * (d[1] + v * d[2]))
            tv.append(h[1] + v2 * h[2])
        return x, tu, tv

    def inner(a, b):
        return a[0] * b[0] + a[1] * b[1] + a[2] * b[2]

    u = v = jnp.zeros_like(point[0])
    for step in range(NEWTON):
        if step == 0:
            x = [coef[c][0][0] for c in range(3)]
            tu = [coef[c][1][0] for c in range(3)]
            tv = [coef[c][0][1] for c in range(3)]
        else:
            x, tu, tv = surface(u, v)
        o = [point[c] - x[c] for c in range(3)]
        a_uu, a_uv, a_vv = inner(tu, tu), inner(tu, tv), inner(tv, tv)
        b_u, b_v = inner(tu, o), inner(tv, o)
        scale = 1.0 / (a_uu * a_vv - a_uv * a_uv)
        du = (a_vv * b_u - a_uv * b_v) * scale
        dv = (a_uu * b_v - a_uv * b_u) * scale
        u = jnp.clip(u + du, -CLIP_EDGE, CLIP_EDGE)
        v = jnp.clip(v + dv, -CLIP_EDGE, CLIP_EDGE)
    x, tu, tv = surface(u, v)
    n = [
        tu[1] * tv[2] - tu[2] * tv[1],
        tu[2] * tv[0] - tu[0] * tv[2],
        tu[0] * tv[1] - tu[1] * tv[0],
    ]
    unit = 1.0 / jnp.sqrt(inner(n, n))
    gap = inner([point[c] - x[c] for c in range(3)], n) * unit
    size = 0.5 * stiff * jnp.maximum(-gap, 0.0) * unit
    return u, v, [size * n[c] for c in range(3)]


def force_body(recv_ref, table_ref, back_ref, uv_ref, force_ref, index_ref, rows_ref):
    for i in range(3):
        rows_ref[i * LANES:(i + 1) * LANES] = recv_ref[pl.ds(i, DEV, stride=3), :].T
    shape = (8, LANES)
    upper = iota(shape, 0) < 4
    force_ref[3 * SK + 3 * MK:] = jnp.zeros((LANES - 32, LANES), F32)
    for g in range(12):
        if g < 8:
            at = [c * SK + g * 8 for c in range(4)]
            out = [c * SK + g * 8 for c in range(3)]
        else:
            at = [4 * SK + c * MK + (g - 8) * 8 for c in range(4)]
            out = [3 * SK + c * MK + (g - 8) * 8 for c in range(3)]
        point = [rows_ref[at[c]:at[c] + 8, :] for c in range(3)]
        code = rows_ref[at[3]:at[3] + 8, :].astype(I32)
        index = jnp.maximum(code - 1, 0)
        lane = index & 127
        high = index >= LANES

        def entry(row, half):
            def tile(t):
                return jnp.broadcast_to(table_ref[row:row + 1, t * LANES:(t + 1) * LANES], shape)

            if g < 8:
                return tile(2 * g + half)
            first = 4 * (g - 8)
            return jnp.where(upper, tile(first + half), tile(first + 2 + half))

        def pick(row):
            got = [jnp.take_along_axis(entry(row, half), lane, axis=1) for half in range(2)]
            return jnp.where(high, got[1], got[0])

        nodes = [[pick(3 * a + c) for c in range(3)] for a in range(9)]
        stiff = jnp.where(code > 0, pick(27), 0.0)
        u, v, force = project(point, nodes, stiff)
        uv_ref[g * 8:g * 8 + 8] = u
        uv_ref[96 + g * 8:96 + g * 8 + 8] = v
        index_ref[g * 8:g * 8 + 8] = index
        for c in range(3):
            force_ref[out[c]:out[c] + 8] = force[c]
    for i in range(3):
        back_ref[pl.ds(i, DEV, stride=3), :] = force_ref[i * LANES:(i + 1) * LANES].T


def forces(recv, table):
    return call(
        force_body,
        (
            jax.ShapeDtypeStruct((3 * DEV, LANES), F32),
            jax.ShapeDtypeStruct((192, LANES), F32),
            jax.ShapeDtypeStruct((3 * LANES, LANES), F32),
            jax.ShapeDtypeStruct((96, LANES), I32),
        ),
        [pltpu.VMEM((3 * LANES, LANES), F32)],
        cost=10**9,
    )(recv, table)


def split(x):
    high = x.astype(BF16)
    return high, (x - high.astype(F32)).astype(BF16)


def react_body(uv_ref, force_ref, index_ref, inv_ref, out_ref, part_ref, sum_ref):
    part_ref[27 * 8:] = jnp.zeros((40, LANES), F32)

    def pieces(g, first, count):
        left, right = [], []
        for k in range(first, first + count):
            left.append(jnp.concatenate(split(part_ref[pl.ds(k, 32, stride=8), :]), 0))
            right.append(one_hot(2 * LANES, index_ref[g * 8 + k:g * 8 + k + 1, :]))
        return dot_nt(jnp.concatenate(left, 1), jnp.concatenate(right, 1))

    def reactions(g):
        u = uv_ref[g * 8:g * 8 + 8]
        v = uv_ref[96 + g * 8:96 + g * 8 + 8]
        lu = (u * (u - 1.0) * 0.5, 1.0 - u * u, u * (u + 1.0) * 0.5)
        lv = (v * (v - 1.0) * 0.5, 1.0 - v * v, v * (v + 1.0) * 0.5)
        for c in range(3):
            row = c * SK + g * 8 if g < 8 else 3 * SK + c * MK + (g - 8) * 8
            f = -force_ref[row:row + 8]
            for j in range(3):
                fj = f * lv[j]
                for i in range(3):
                    a = 3 * (i + 3 * j) + c
                    part_ref[a * 8:a * 8 + 8] = lu[i] * fj

    mirrored = []
    for m in range(4):
        reactions(8 + m)
        mirrored += [pieces(8 + m, 0, 4), pieces(8 + m, 4, 4)]
        for b in (2 * m, 2 * m + 1):
            reactions(b)
            both = mirrored[b] + pieces(b, 0, 8)
            sum_ref[:, b * 256:(b + 1) * 256] = both[0:32] + both[32:64]

    for m in range(FT):
        hi = inv_ref[m:m + 1, :]
        lane = jnp.broadcast_to(inv_ref[FT + m:FT + m + 1, :], (8, LANES))
        tile = jnp.broadcast_to(hi, (8, LANES))
        at_tile = [tile == t for t in range(FT)]
        for g in range(4):
            out = jnp.zeros((8, LANES), F32)
            for t in range(FT):
                got = jnp.take_along_axis(
                    sum_ref[8 * g:8 * g + 8, t * LANES:(t + 1) * LANES], lane, axis=1
                )
                out = jnp.where(at_tile[t], got, out)
            out_ref[8 * g:8 * g + 8, m * LANES:(m + 1) * LANES] = out


def react(uv, force, index, inv):
    return call(
        react_body,
        jax.ShapeDtypeStruct((32, FT * LANES), F32),
        [
            pltpu.VMEM((256, LANES), F32),
            pltpu.VMEM((32, FT * LANES), F32),
        ],
        cost=10**9,
    )(uv, force, index, inv)


def finish_body(
    back_ref, speer_ref, sk_ref, mpeer_ref, mk_ref, mface_ref, mnode_ref, part_ref,
    slave_ref, face_ref, rows_ref, own_ref,
):
    for i in range(3):
        rows_ref[i * LANES:(i + 1) * LANES] = back_ref[pl.ds(i, DEV, stride=3), :].T

    def collect(peer, slot, base, slots):
        at_slot = [slot == k for k in range(slots)]
        for c in range(3):
            out = jnp.zeros((8, LANES), F32)
            for k in range(slots):
                row = base + c * slots + k
                out = jnp.where(at_slot[k], row_gather(rows_ref[row:row + 1, :], peer, (8, LANES)), out)
            yield c, out

    for m in range(MB // 8):
        for c, out in collect(mpeer_ref[8 * m:8 * m + 8], mk_ref[8 * m:8 * m + 8], 3 * SK, MK):
            own_ref[c, 8 * m:8 * m + 8] = out

    sub = iota((32, LANES), 0)
    comp = sub % 3
    node = sub // 3
    zero = jnp.zeros((64, LANES), BF16)
    both = jnp.zeros((8 * 64, 2 * LANES), F32)
    left, right = [], []
    for r in range(MB):
        f = jnp.where(comp == 0, own_ref[0, r:r + 1, :], own_ref[1, r:r + 1, :])
        f = jnp.where(comp == 2, own_ref[2, r:r + 1, :], f)
        f = jnp.where(node == mnode_ref[r:r + 1, :], f, 0.0)
        f = jnp.concatenate(split(f), 0)
        face = mface_ref[r:r + 1, :]
        high = wide16(face >> 8, 64)
        left.append(jnp.concatenate(
            [jnp.where(high == jnp.full((64, LANES), h, I16), f, zero) for h in range(8)], 0
        ))
        right.append(one_hot(2 * LANES, face & 255))
        if r % 2 == 1:
            both = both + dot_nt(jnp.concatenate(left, 1), jnp.concatenate(right, 1))
            left, right = [], []
    for h in range(8):
        at = slice(h * 256, (h + 1) * 256)
        share = both[64 * h:64 * h + 32] + both[64 * h + 32:64 * h + 64]
        face_ref[:, at] = (part_ref[:, at] + share)[0:27]

    for m in range(SB // 8):
        for c, out in collect(speer_ref[8 * m:8 * m + 8], sk_ref[8 * m:8 * m + 8], 0, SK):
            for r in range(8):
                at = (8 * m + r) * LANES
                slave_ref[c:c + 1, at:at + LANES] = out[r:r + 1, :]


def finish(back, speer, sk, mpeer, mk, mface, mnode, part):
    return call(
        finish_body,
        (
            jax.ShapeDtypeStruct((3, SB * LANES), F32),
            jax.ShapeDtypeStruct((27, FT * LANES), F32),
        ),
        [
            pltpu.VMEM((3 * LANES, LANES), F32),
            pltpu.VMEM((3, MB, LANES), F32),
        ],
        cost=10**9,
    )(back, speer, sk, mpeer, mk, mface, mnode, part)


def exchange(x):
    x = x.reshape(DEV, 1, 3 * LANES)
    x = lax.all_to_all(x, ("mech", "bin"), split_axis=0, concat_axis=0, tiled=True)
    return x.reshape(3 * DEV, LANES)


def shards(
    face_coords, face_stiff, bin_order, slave_pos, slave_dest, face_slot, block_count,
    mirror_face, mirror_node, mirror_dest, mirror_slot,
):
    mface = mirror_face.reshape(MB, LANES)
    mnode = mirror_node.reshape(MB, LANES)
    send, speer, sk, mpeer, mk = pack(
        block_count,
        slave_dest.reshape(SB, LANES),
        face_slot.reshape(SB, LANES),
        slave_pos,
        mirror_dest.reshape(MB, LANES),
        mirror_slot.reshape(MB, LANES),
        mface,
        mnode,
        face_coords,
    )
    recv = exchange(send)
    table, inv = order_faces(
        face_coords, face_stiff.reshape(1, FT * LANES), bin_order.reshape(FT, LANES)
    )
    back, uv, force, index = forces(recv, table)
    returned = exchange(back)
    part = react(uv, force, index, inv)
    return finish(returned, speer, sk, mpeer, mk, mface, mnode, part)


def solution(mesh):
    axes = ("mech", "bin")
    return jax.shard_map(
        shards,
        mesh=mesh,
        in_specs=(
            P(None, axes), P(axes), P(axes, None), P(None, axes), P(axes, None), P(axes),
            P(axes, None), P(axes), P(axes), P(axes, None), P(axes),
        ),
        out_specs=(P(None, axes), P(None, axes)),
        check_vma=False,
    )
```

time: 64.7 us -> 53.4 us (0.83)
  Pallas kernels: 36.4 us -> 13.3 us
  waiting for transfers between devices: 4.75 us -> 16.9 us
  starting transfers between devices: 21.3 us -> 15.9 us
  local copies, waits for them, and re-layouts: 1.37 us -> 6.02 us
    all_to_all x2, waiting for transfers between devices: 4.75 us -> 16.9 us  [exchange(): lax.all_to_all(x, ('mech', 'bin'), split_axis=0, concat_axis=0, tiled=True)]
    pallas_call x1, Pallas kernels: 10.5 us -> 1.21 us  [order_faces(): call(order_body, (jax.ShapeDtypeStruct((32, faces), F32), jax.ShapeDtypeS...]
    pallas_call x1, Pallas kernels: 7.29 us -> 1.87 us  [finish(): call(finish_body, (jax.ShapeDtypeStruct((3, SB * LANES), F32), jax.ShapeD...]
    all_to_all x2, starting transfers between devices: 21.3 us -> 15.9 us  [exchange(): lax.all_to_all(x, ('mech', 'bin'), split_axis=0, concat_axis=0, tiled=True)]
    unnamed x4 -> x28, local copies, waits for them, and re-layouts: 1.37 us -> 6.02 us
    pallas_call x1, Pallas kernels: 9.37 us -> 5.12 us  [pack(): call(pack_body, (jax.ShapeDtypeStruct((3 * DEV, LANES), F32), jax.ShapeDt...]
    pallas_call x1, Pallas kernels: 5.62 us -> 2.64 us  [react(): call(react_body, jax.ShapeDtypeStruct((32, FT * LANES), F32), [pltpu.VMEM...]
    pallas_call x1, Pallas kernels: 3.55 us -> 2.47 us  [forces(): call(force_body, (jax.ShapeDtypeStruct((3 * DEV, LANES), F32), jax.ShapeD...]
  transfers between devices with their start and end apart: 2 -> 2, of which waited for: 1 -> 2; matrix products, arithmetic and copies ran while one was open for 0% -> 0% of each run, Pallas kernels for 25% -> 7%
where the time goes in v1:
time: 53.4 us; the launch traced here: 52.8 us
  waiting for transfers between devices  16.9 us (32%)
  starting transfers between devices  15.9 us (30%)
  Pallas kernels  13.3 us (25%)
  local copies, waits for them, and re-layouts  6.02 us (11%)
  between operations  0.73 us (1%)
    all_to_all x2, waiting for transfers between devices, exchange(): lax.all_to_all(x, ('mech', 'bin'), split_axis=0, concat_axis=0, tiled=True)  16.9 us
    all_to_all x2, starting transfers between devices, exchange(): lax.all_to_all(x, ('mech', 'bin'), split_axis=0, concat_axis=0, tiled=True)  15.9 us
    unnamed x28, local copies, waits for them, and re-layouts  6.02 us
    pallas_call x1, Pallas kernels, pack(): call(pack_body, (jax.ShapeDtypeStruct((3 * DEV, LANES), F32), jax.ShapeDt...  5.12 us
    pallas_call x1, Pallas kernels, react(): call(react_body, jax.ShapeDtypeStruct((32, FT * LANES), F32), [pltpu.VMEM...  2.64 us
    pallas_call x1, Pallas kernels, forces(): call(force_body, (jax.ShapeDtypeStruct((3 * DEV, LANES), F32), jax.ShapeD...  2.47 us
    pallas_call x1, Pallas kernels, finish(): call(finish_body, (jax.ShapeDtypeStruct((3, SB * LANES), F32), jax.ShapeD...  1.87 us
    pallas_call x1, Pallas kernels, order_faces(): call(order_body, (jax.ShapeDtypeStruct((32, faces), F32), jax.ShapeDtypeS...  1.21 us
  transfers between devices with their start and end apart: 2, of which 2 were waited for; matrix products, arithmetic and copies ran while one was open for 0% of the time, Pallas kernels for 7%

profile of v1, /device:TPU:1, one launch (start us, length us, event | category | flops | bytes accessed | tf_op | source)
XLA Modules:
  0.0 52.8 jit_solution(6818852993882634412)
XLA Ops:
  0.6 0.0 copy-start.5
  0.6 0.0 copy-start.13
  0.7 0.7 %copy-done.5 = s32[2048,1]{0,1:T(1,128)S(1)} copy-done((s32[2048,1]{0,1:T(1,128)S(1)}, s32[2048,1]{0,1:T(1,128)}, u32[]{:S(2)}) %copy-start.5) | copy-done | bytes 8216
  1.3 0.0 copy-done.13
  1.3 0.0 copy-start
  1.3 0.9 %copy-done = f32[27,2048]{1,0:T(8,128)S(1)} copy-done((f32[27,2048]{1,0:T(8,128)S(1)}, f32[27,2048]{1,0:T(8,128)}, u32[]{:S(2)}) %copy-start) | copy-done | bytes 221208
  2.3 0.0 copy-start.2
  2.3 0.8 %copy-done.2 = f32[3,4096]{1,0:T(4,128)S(1)} copy-done((f32[3,4096]{1,0:T(4,128)S(1)}, f32[3,4096]{1,0:T(4,128)}, u32[]{:S(2)}) %copy-start.2) | copy-done | bytes 49176
  3.1 0.0 copy-start.3
  3.1 0.7 %copy-done.3 = s32[4096,1]{0,1:T(1,128)S(1)} copy-done((s32[4096,1]{0,1:T(1,128)S(1)}, s32[4096,1]{0,1:T(1,128)}, u32[]{:S(2)}) %copy-start.3) | copy-done | bytes 16408
  3.8 0.0 copy-start.4
  3.8 0.7 %copy-done.4 = s32[4096]{0:T(1024)S(1)} copy-done((s32[4096]{0:T(1024)S(1)}, s32[4096]{0:T(1024)}, u32[]{:S(2)}) %copy-start.4) | copy-done | bytes 16408
  4.6 0.0 copy-start.6
  4.6 0.7 %copy-done.6 = s32[2048]{0:T(1024)S(1)} copy-done((s32[2048]{0:T(1024)S(1)}, s32[2048]{0:T(1024)}, u32[]{:S(2)}) %copy-start.6) | copy-done | bytes 8216
  5.3 0.7 %copy-done.9 = s32[2048]{0:T(1024)S(1)} copy-done((s32[2048]{0:T(1024)S(1)}, s32[2048]{0:T(1024)}, u32[]{:S(2)}) %copy-start.9) | copy-done | bytes 8216
  6.0 0.7 %copy-done.11 = s32[2048]{0:T(1024)S(1)} copy-done((s32[2048]{0:T(1024)S(1)}, s32[2048]{0:T(1024)}, u32[]{:S(2)}) %copy-start.11) | copy-done | bytes 8216
  6.7 5.1 %shard_map.122 = (f32[384,128]{1,0:T(8,128)}, s32[32,128]{1,0:T(8,128)S(1)}, s32[32,128]{1,0:T(8,128)S(1)}, s32[16,128]{1,0:T(8,128)S(1)}, s32[16,128]{1,0:T(8,128)S(1)}) custom-call(s32[1,32]{1,0:T(1,128)S(1)} %copy-done.13, s32[32,128]{1,0:T(8,128)S(1)} %bitcast.14, s32[32,128]{1,0:T(8,128)S(1)} %bitcast.15, f32[3,4096]{1,0:T(4,128)S(1)} %copy-done.2, ...), custom_call_target="tpu_custom_call" | custom-call | flops 1000000000 | bytes 10000000 | tf_op jit(solution)/shard_map/pallas_call | solution.py:190
  11.8 11.5 %all-to-all-start = ((f32[128,1,384]{2,1,0:T(1,128)}), f32[128,1,384]{2,1,0:T(1,128)S(1)}, u32[]{:S(2)}, u32[]{:S(2)}) async-start(f32[128,1,384]{2,1,0:T(1,128)} %bitcast.6), calls=%async_computation | async-start | bytes 393216 | tf_op jit(solution)/shard_map/all_to_all | solution.py:508
  23.3 0.0 copy-done.1
  23.3 0.0 copy-done.7
  23.3 0.0 copy-done.8
  23.3 1.2 %shard_map.123 = (f32[32,2048]{1,0:T(8,128)S(1)}, s32[32,128]{1,0:T(8,128)S(1)}) custom-call(f32[27,2048]{1,0:T(8,128)S(1)} %copy-done.1, f32[1,2048]{1,0:T(1,128)S(1)} %bitcast.18, s32[16,128]{1,0:T(8,128)S(1)} %bitcast.19), custom_call_target="tpu_custom_call" | custom-call | flops 1000000000 | bytes 10000000 | tf_op jit(solution)/shard_map/pallas_call | solution.py:251
  24.5 9.1 %all-to-all-done = f32[128,1,384]{2,1,0:T(1,128)S(1)} async-done(((f32[128,1,384]{2,1,0:T(1,128)}), f32[128,1,384]{2,1,0:T(1,128)S(1)}, u32[]{:S(2)}, u32[]{:S(2)}) %all-to-all-start) | async-done | bytes 196640 | tf_op jit(solution)/shard_map/all_to_all | solution.py:508
  33.7 2.5 %shard_map.124 = (f32[384,128]{1,0:T(8,128)}, f32[192,128]{1,0:T(8,128)S(1)}, f32[384,128]{1,0:T(8,128)S(1)}, s32[96,128]{1,0:T(8,128)S(1)}) custom-call(f32[384,128]{1,0:T(8,128)S(1)} %bitcast.13, f32[32,2048]{1,0:T(8,128)S(1)} %get-tuple-element.14.table_ref), custom_call_target="tpu_custom_call" | custom-call | flops 1000000000 | bytes 10000000 | tf_op jit(solution)/shard_map/pallas_call | solution.py:361
  36.1 4.4 %all-to-all-start.1 = ((f32[128,1,384]{2,1,0:T(1,128)}), f32[128,1,384]{2,1,0:T(1,128)S(1)}, u32[]{:S(2)}, u32[]{:S(2)}) async-start(f32[128,1,384]{2,1,0:T(1,128)} %bitcast.10), calls=%async_computation.1 | async-start | bytes 393216 | tf_op jit(solution)/shard_map/all_to_all | solution.py:508
  40.6 0.0 copy-start.12
  40.6 2.6 %shard_map.125.part_ref = f32[32,2048]{1,0:T(8,128)S(1)} custom-call(f32[192,128]{1,0:T(8,128)S(1)} %get-tuple-element.20.uv_ref, f32[384,128]{1,0:T(8,128)S(1)} %get-tuple-element.21.force_ref, s32[96,128]{1,0:T(8,128)S(1)} %get-tuple-element.22.index_ref, s32[32,128]{1,0:T(8,128)S(1)} %get-tuple-element.23.inv_ref), custom_call_target="tpu_custom_call" | custom-call | flops 1000000000 | bytes 10000000 | tf_op jit(solution)/shard_map/pallas_call | solution.py:428
  43.2 0.0 copy-start.10
  43.2 7.7 %all-to-all-done.1 = f32[128,1,384]{2,1,0:T(1,128)S(1)} async-done(((f32[128,1,384]{2,1,0:T(1,128)}), f32[128,1,384]{2,1,0:T(1,128)S(1)}, u32[]{:S(2)}, u32[]{:S(2)}) %all-to-all-start.1) | async-done | bytes 196640 | tf_op jit(solution)/shard_map/all_to_all | solution.py:508
  51.0 0.0 copy-done.12
  51.0 0.0 copy-done.10
  51.0 1.9 %shard_map.126 = (f32[3,4096]{1,0:T(4,128)}, f32[27,2048]{1,0:T(8,128)}) custom-call(f32[384,128]{1,0:T(8,128)S(1)} %bitcast.12, s32[32,128]{1,0:T(8,128)S(1)} %get-tuple-element.16.speer_ref, s32[32,128]{1,0:T(8,128)S(1)} %get-tuple-element.17.sk_ref, s32[16,128]{1,0:T(8,128)S(1)} %get-tuple-element.18.mpeer_ref, s32[16,128]{1,0:T(8,128)S(1)} %get-tuple-element.19.mk_ref, ...), custom_call_target="tpu_custom_call" | custom-call | flops 1000000000 | bytes 10000000 | tf_op jit(solution)/shard_map/pallas_call | solution.py:492
  (5 shorter events, 0.0 us)
Async XLA Ops:
  0.6 0.7 %copy-start.5 = (s32[2048,1]{0,1:T(1,128)S(1)}, s32[2048,1]{0,1:T(1,128)}, u32[]{:S(2)}) copy-start(s32[2048,1]{0,1:T(1,128)} %param.20) | copy-start | bytes 24580
  0.6 0.7 %copy-start.13 = (s32[1,32]{1,0:T(1,128)S(1)}, s32[1,32]{1,0:T(1,128)}, u32[]{:S(2)}) copy-start(s32[1,32]{1,0:T(1,128)} %count_ref.1) | copy-start | bytes 388
  1.3 1.0 %copy-start = (f32[27,2048]{1,0:T(8,128)S(1)}, f32[27,2048]{1,0:T(8,128)}, u32[]{:S(2)}) copy-start(f32[27,2048]{1,0:T(8,128)} %coords_ref.3) | copy-start | bytes 663556
  2.3 0.8 %copy-start.2 = (f32[3,4096]{1,0:T(4,128)S(1)}, f32[3,4096]{1,0:T(4,128)}, u32[]{:S(2)}) copy-start(f32[3,4096]{1,0:T(4,128)} %spos_ref.1) | copy-start | bytes 147460
  3.1 0.7 %copy-start.3 = (s32[4096,1]{0,1:T(1,128)S(1)}, s32[4096,1]{0,1:T(1,128)}, u32[]{:S(2)}) copy-start(s32[4096,1]{0,1:T(1,128)} %param.15) | copy-start | bytes 49156
  3.8 0.7 %copy-start.4 = (s32[4096]{0:T(1024)S(1)}, s32[4096]{0:T(1024)}, u32[]{:S(2)}) copy-start(s32[4096]{0:T(1024)} %param.16) | copy-start | bytes 49156
  4.6 0.7 %copy-start.6 = (s32[2048]{0:T(1024)S(1)}, s32[2048]{0:T(1024)}, u32[]{:S(2)}) copy-start(s32[2048]{0:T(1024)} %param.21) | copy-start | bytes 24580
  5.3 0.7 %copy-start.9 = (s32[2048]{0:T(1024)S(1)}, s32[2048]{0:T(1024)}, u32[]{:S(2)}) copy-start(s32[2048]{0:T(1024)} %param.18) | copy-start | bytes 24580
  6.0 0.7 %copy-start.11 = (s32[2048]{0:T(1024)S(1)}, s32[2048]{0:T(1024)}, u32[]{:S(2)}) copy-start(s32[2048]{0:T(1024)} %param.19) | copy-start | bytes 24580
  11.8 11.5 %copy-start.1 = (f32[27,2048]{1,0:T(8,128)S(1)}, f32[27,2048]{1,0:T(8,128)}, u32[]{:S(2)}) copy-start(f32[27,2048]{1,0:T(8,128)} %coords_ref.3) | copy-start | bytes 663556
  11.8 11.5 %copy-start.7 = (f32[2048]{0:T(1024)S(1)}, f32[2048]{0:T(1024)}, u32[]{:S(2)}) copy-start(f32[2048]{0:T(1024)} %param.12) | copy-start | bytes 24580
  11.8 11.5 %copy-start.8 = (s32[1,2048]{1,0:T(1,128)S(1)}, s32[1,2048]{1,0:T(1,128)}, u32[]{:S(2)}) copy-start(s32[1,2048]{1,0:T(1,128)} %param.13) | copy-start | bytes 24580
  11.8 21.9 %all-to-all-start = ((f32[128,1,384]{2,1,0:T(1,128)}), f32[128,1,384]{2,1,0:T(1,128)S(1)}, u32[]{:S(2)}, u32[]{:S(2)}) async-start(f32[128,1,384]{2,1,0:T(1,128)} %bitcast.6), calls=%async_computation | async-start | bytes 393216 | tf_op jit(solution)/shard_map/all_to_all | solution.py:508
  36.1 14.8 %all-to-all-start.1 = ((f32[128,1,384]{2,1,0:T(1,128)}), f32[128,1,384]{2,1,0:T(1,128)S(1)}, u32[]{:S(2)}, u32[]{:S(2)}) async-start(f32[128,1,384]{2,1,0:T(1,128)} %bitcast.10), calls=%async_computation.1 | async-start | bytes 393216 | tf_op jit(solution)/shard_map/all_to_all | solution.py:508
  40.6 10.4 %copy-start.12 = (s32[2048]{0:T(1024)S(1)}, s32[2048]{0:T(1024)}, u32[]{:S(2)}) copy-start(s32[2048]{0:T(1024)} %param.19) | copy-start | bytes 24580
  43.2 7.7 %copy-start.10 = (s32[2048]{0:T(1024)S(1)}, s32[2048]{0:T(1024)}, u32[]{:S(2)}) copy-start(s32[2048]{0:T(1024)} %param.18) | copy-start | bytes 24580

commit v2 on v1

--- a/solution.py
+++ b/solution.py
@@ -54,13 +54,13 @@
     return jnp.take_along_axis(jnp.broadcast_to(row, shape), lane, axis=1)
 
 
-def call(body, out_shape, scratch=(), in_specs=None, cost=0):
+def call(body, out_shape, scratch=(), in_specs=None, cost=0, vmem=VMEM_BYTES):
     kwargs = {} if in_specs is None else {"in_specs": in_specs}
     return pl.pallas_call(
         body,
         out_shape=out_shape,
         scratch_shapes=list(scratch),
-        compiler_params=pltpu.CompilerParams(vmem_limit_bytes=VMEM_BYTES),
+        compiler_params=pltpu.CompilerParams(vmem_limit_bytes=vmem),
         cost_estimate=pl.CostEstimate(flops=cost, bytes_accessed=cost // 100, transcendentals=0),
         **kwargs,
     )
@@ -68,13 +68,25 @@
 
 VM = pl.BlockSpec(memory_space=pltpu.VMEM)
 SM = pl.BlockSpec(memory_space=pltpu.SMEM)
+HB = pl.BlockSpec(memory_space=pltpu.HBM)
 
 
 def pack_body(
-    count_ref, sdest_ref, sslot_ref, spos_ref, mdest_ref, mslot_ref, mface_ref, mnode_ref, coords_ref,
-    send_ref, speer_ref, sk_ref, mpeer_ref, mk_ref,
-    cell_ref, e_ref, b_ref, code_ref, turn_ref, cols_ref, cnt_ref, pts_ref, rows_ref,
+    count_ref, *refs,
 ):
+    sources, refs = refs[:8], refs[8:]
+    send_ref, speer_ref, sk_ref, mpeer_ref, mk_ref = refs[:5]
+    buffers, refs = refs[5:13], refs[13:]
+    sdest_ref, sslot_ref, mdest_ref, mslot_ref, mface_ref, mnode_ref, coords_ref, spos_ref = buffers
+    e_ref, b_ref, val_ref, turn_ref, cols_ref, cnt_ref, rows_ref, sems = refs
+    copies = [
+        pltpu.make_async_copy(sources[i], buffers[i], sems.at[i]) for i in range(8)
+    ]
+    for copy in copies:
+        copy.start()
+    for copy in copies:
+        copy.wait()
+
     def keys(dest, slot):
         owner = (dest & ~(NBIN - 1)) | (slot >> 8)
         return owner, dest & (NBIN - 1), (slot & 255) + 1
@@ -87,10 +99,9 @@
         owner, col, code = keys(dest_ref[...], slot_ref[...])
         e_ref[first:first + rows] = owner
         b_ref[first:first + rows] = col
-        code_ref[first:first + rows] = code.astype(F32)
+        val_ref[6, first:first + rows] = code.astype(F32)
         peer_ref[...] = owner
         cell = (owner * NBIN + col).astype(F32)
-        cell_ref[first:first + rows] = cell
         turn_ref[first:first + rows] = cell
         turn_ref[half + first:half + first + rows] = pltpu.roll(cell, half, axis=1)
     for first in (SB + MB, half + SB + MB):
@@ -104,46 +115,10 @@
     upper = lane8 >= half
     row16 = iota((16, LANES), 0)
     bin_rows = jnp.where((row16 < 8) | (iota((16, LANES), 1) < half), row16 & 7, -1).astype(I16)
-    lanes_bf = iota((64, LANES), 1).astype(F32).astype(BF16)
 
     for r in range(SB + MB):
         bins = pick_bf16(bin_rows, b_ref[r:r + 1, :])
         cnt_ref[r] = dot_nt(bins, one_hot(LANES, e_ref[r:r + 1, :]))
-
-    def slots(first, last, cap, rows, kout):
-        seen = jnp.zeros((NBIN, LANES), F32)
-        inverse = jnp.zeros((2 * rows, LANES), F32)
-        for group in range(first, last, 4):
-            left, right = [], []
-            for r in range(group, group + 4):
-                i = r - first
-                peers = jnp.broadcast_to(e_ref[r:r + 1, :], (NBIN, LANES))
-                column = jnp.where(upper, half + r, r)
-                before = jnp.take_along_axis(seen, peers, axis=1) + jnp.where(
-                    upper, jnp.take_along_axis(cnt_ref[r, 8:16], peers, axis=1), 0.0
-                )
-                before = jnp.where(sub8 == b_ref[r:r + 1, :], before, 0.0)
-                for m in range(half // 8):
-                    col = jnp.take_along_axis(cols_ref[8 * m:8 * m + 8], column, axis=1)
-                    same = (cell_ref[r:r + 1, :] == col) & earlier[8 * m:8 * m + 8]
-                    before = before + jnp.where(same, 1.0, 0.0)
-                rank = jnp.sum(before, 0, keepdims=True)
-                k = b_ref[r:r + 1, :] * cap + rank.astype(I32)
-                if first == 0:
-                    k = jnp.where(lane_row < count_ref[0, i], k, -1)
-                kout[i:i + 1, :] = k
-                mine = slot_rows(rows) == wide16(k, rows)
-                left.append(jnp.concatenate([
-                    jnp.where(mine, jnp.full((rows, LANES), i + 1, BF16), jnp.zeros((rows, LANES), BF16)),
-                    jnp.where(mine, lanes_bf[:rows], jnp.zeros((rows, LANES), BF16)),
-                ], 0))
-                right.append(one_hot(LANES, e_ref[r:r + 1, :]))
-                seen = seen + cnt_ref[r, 0:8]
-            inverse = inverse + dot_nt(jnp.concatenate(left, 1), jnp.concatenate(right, 1))
-        return inverse
-
-    sinv = slots(0, SB, 8, SK, sk_ref)
-    minv = slots(SB, SB + MB, 4, MK, mk_ref)
 
     for m in range(MB // 8):
         face = mface_ref[8 * m:8 * m + 8]
@@ -161,32 +136,60 @@
                     )
                     part = jnp.where(at_tile[t], got, part)
                 point = jnp.where(node == n, part, point)
-            pts_ref[c, 8 * m:8 * m + 8] = point
-
-    for blocks, rows, inverse, base in ((SB, SK, sinv, 0), (MB, MK, minv, 4 * SK)):
-        for m in range(rows // 8):
-            source = inverse[8 * m:8 * m + 8].astype(I32) - 1
-            lane = inverse[rows + 8 * m:rows + 8 * m + 8].astype(I32)
-            at_block = [source == r for r in range(blocks)]
-            for c in range(4):
-                out = jnp.zeros((8, LANES), F32)
-                for r in range(blocks):
-                    if c == 3:
-                        first = 0 if base == 0 else SB
-                        row = code_ref[first + r:first + r + 1, :]
-                    elif base == 0:
-                        row = spos_ref[c:c + 1, r * LANES:(r + 1) * LANES]
-                    else:
-                        row = pts_ref[c, r:r + 1, :]
-                    out = jnp.where(at_block[r], row_gather(row, lane, (8, LANES)), out)
-                at = base + c * rows + 8 * m
-                rows_ref[at:at + 8] = out
+            high = point.astype(BF16).astype(F32)
+            val_ref[c, SB + 8 * m:SB + 8 * m + 8] = high
+            val_ref[3 + c, SB + 8 * m:SB + 8 * m + 8] = point - high
+
+    def value(i, r):
+        if r >= SB or i == 6:
+            return val_ref[i, r:r + 1, :]
+        x = spos_ref[i % 3:i % 3 + 1, r * LANES:(r + 1) * LANES]
+        high = x.astype(BF16).astype(F32)
+        return high if i < 3 else x - high
+
+    def slots(first, last, cap, rows, kout):
+        seen = jnp.zeros((NBIN, LANES), F32)
+        total = jnp.zeros((7 * rows, LANES), F32)
+        zero = jnp.zeros((rows, LANES), BF16)
+        for group in range(first, last, 4):
+            left, right = [], []
+            for r in range(group, group + 4):
+                i = r - first
+                peers = jnp.broadcast_to(e_ref[r:r + 1, :], (NBIN, LANES))
+                column = jnp.where(upper, half + r, r)
+                before = jnp.take_along_axis(seen, peers, axis=1) + jnp.where(
+                    upper, jnp.take_along_axis(cnt_ref[r, 8:16], peers, axis=1), 0.0
+                )
+                before = jnp.where(sub8 == b_ref[r:r + 1, :], before, 0.0)
+                for m in range(half // 8):
+                    col = jnp.take_along_axis(cols_ref[8 * m:8 * m + 8], column, axis=1)
+                    same = (turn_ref[r:r + 1, :] == col) & earlier[8 * m:8 * m + 8]
+                    before = before + jnp.where(same, 1.0, 0.0)
+                rank = jnp.sum(before, 0, keepdims=True)
+                k = b_ref[r:r + 1, :] * cap + rank.astype(I32)
+                if first == 0:
+                    k = jnp.where(lane_row < count_ref[0, i], k, -1)
+                kout[i:i + 1, :] = k
+                mine = slot_rows(rows) == wide16(k, rows)
+                parts = []
+                for j in (0, 1, 2, 6, 3, 4, 5):
+                    x = jnp.broadcast_to(value(j, r), (16, LANES)).astype(BF16)
+                    parts.append(jnp.where(mine, jnp.concatenate([x] * (rows // 16), 0), zero))
+                left.append(jnp.concatenate(parts, 0))
+                right.append(one_hot(LANES, e_ref[r:r + 1, :]))
+                seen = seen + cnt_ref[r, 0:8]
+            total = total + dot_nt(jnp.concatenate(left, 1), jnp.concatenate(right, 1))
+        return jnp.concatenate([total[0:3 * rows] + total[4 * rows:], total[3 * rows:4 * rows]], 0)
+
+    rows_ref[0:4 * SK] = slots(0, SB, 8, SK, sk_ref)
+    rows_ref[4 * SK:] = slots(SB, SB + MB, 4, MK, mk_ref)
     for i in range(3):
         send_ref[pl.ds(i, DEV, stride=3), :] = rows_ref[i * LANES:(i + 1) * LANES].T
 
 
 def pack(count, sdest, sslot, spos, mdest, mslot, mface, mnode, coords):
     blocks = SB + MB
+    arrays = (sdest, sslot, mdest, mslot, mface, mnode, coords, spos)
     return call(
         pack_body,
         (
@@ -196,24 +199,34 @@
             jax.ShapeDtypeStruct((MB, LANES), I32),
             jax.ShapeDtypeStruct((MB, LANES), I32),
         ),
-        [
-            pltpu.VMEM((blocks, LANES), F32),
+        [pltpu.VMEM(x.shape, x.dtype) for x in arrays] + [
             pltpu.VMEM((blocks, LANES), I32),
             pltpu.VMEM((blocks, LANES), I32),
-            pltpu.VMEM((blocks, LANES), F32),
+            pltpu.VMEM((7, blocks, LANES), F32),
             pltpu.VMEM((LANES, LANES), F32),
             pltpu.VMEM((LANES, LANES), F32),
             pltpu.VMEM((blocks, 16, LANES), F32),
-            pltpu.VMEM((3, MB, LANES), F32),
             pltpu.VMEM((3 * LANES, LANES), F32),
+            pltpu.SemaphoreType.DMA((8,)),
         ],
-        in_specs=[SM] + [VM] * 8,
+        in_specs=[SM] + [HB] * 8,
         cost=10**9,
-    )(count, sdest, sslot, spos, mdest, mslot, mface, mnode, coords)
+        vmem=60 * 1024 * 1024,
+    )(count, *arrays)
+
+
+def quadratic(low, mid, high):
+    return mid, 0.5 * (high - low), 0.5 * (high + low) - mid
 
 
 def order_body(coords_ref, stiff_ref, order_ref, table_ref, inv_ref, src_ref):
-    src_ref[0:27] = coords_ref[...]
+    for c in range(3):
+        node = [coords_ref[3 * a + c:3 * a + c + 1, :] for a in range(9)]
+        by_j = [quadratic(*node[3 * j:3 * j + 3]) for j in range(3)]
+        for p in range(3):
+            for q, value in enumerate(quadratic(by_j[0][p], by_j[1][p], by_j[2][p])):
+                row = 9 * c + 3 * p + q
+                src_ref[row:row + 1] = value
     src_ref[27:28] = stiff_ref[...]
     src_ref[28:32] = jnp.zeros((4, FT * LANES), F32)
     lanes_bf = iota((FT, LANES), 1).astype(F32).astype(BF16)
@@ -259,16 +272,7 @@
     )(coords, stiff, order)
 
 
-def quadratic(low, mid, high):
-    return mid, 0.5 * (high - low), 0.5 * (high + low) - mid
-
-
-def project(point, nodes, stiff):
-    coef = []
-    for c in range(3):
-        by_j = [quadratic(nodes[3 * j][c], nodes[3 * j + 1][c], nodes[3 * j + 2][c]) for j in range(3)]
-        coef.append([quadratic(by_j[0][p], by_j[1][p], by_j[2][p]) for p in range(3)])
-
+def project(point, coef, stiff):
     def surface(u, v):
         u2 = u + u
         v2 = v + v
@@ -345,9 +349,9 @@
             got = [jnp.take_along_axis(entry(row, half), lane, axis=1) for half in range(2)]
             return jnp.where(high, got[1], got[0])
 
-        nodes = [[pick(3 * a + c) for c in range(3)] for a in range(9)]
+        coef = [[[pick(9 * c + 3 * p + q) for q in range(3)] for p in range(3)] for c in range(3)]
         stiff = jnp.where(code > 0, pick(27), 0.0)
-        u, v, force = project(point, nodes, stiff)
+        u, v, force = project(point, coef, stiff)
         uv_ref[g * 8:g * 8 + 8] = u
         uv_ref[96 + g * 8:96 + g * 8 + 8] = v
         index_ref[g * 8:g * 8 + 8] = index

time: 53.4 us -> 46.9 us (0.88)
  local copies, waits for them, and re-layouts: 6.02 us -> 0.05 us
    unnamed x28 -> x18, local copies, waits for them, and re-layouts: 6.02 us -> 0.05 us
  transfers between devices with their start and end apart: 2 -> 2, of which waited for: 2 -> 2; matrix products, arithmetic and copies ran while one was open for 0% -> 0% of each run, Pallas kernels for 7% -> 8%
where the time goes in v2:
time: 46.9 us; the launch traced here: 46.6 us
  waiting for transfers between devices  16.8 us (36%)
  starting transfers between devices  15.9 us (34%)
  Pallas kernels  13.1 us (28%)
  between operations  0.79 us (2%)
    all_to_all x2, waiting for transfers between devices, exchange(): lax.all_to_all(x, ('mech', 'bin'), split_axis=0, concat_axis=0, tiled=True)  16.8 us
    all_to_all x2, starting transfers between devices, exchange(): lax.all_to_all(x, ('mech', 'bin'), split_axis=0, concat_axis=0, tiled=True)  15.9 us
    pallas_call x1, Pallas kernels, pack(): call(pack_body, (jax.ShapeDtypeStruct((3 * DEV, LANES), F32), jax.ShapeDt...  5.06 us
    pallas_call x1, Pallas kernels, react(): call(react_body, jax.ShapeDtypeStruct((32, FT * LANES), F32), [pltpu.VMEM...  2.64 us
    pallas_call x1, Pallas kernels, forces(): call(force_body, (jax.ShapeDtypeStruct((3 * DEV, LANES), F32), jax.ShapeD...  2.28 us
    pallas_call x1, Pallas kernels, finish(): call(finish_body, (jax.ShapeDtypeStruct((3, SB * LANES), F32), jax.ShapeD...  1.87 us
    pallas_call x1, Pallas kernels, order_faces(): call(order_body, (jax.ShapeDtypeStruct((32, faces), F32), jax.ShapeDtypeS...  1.24 us
  transfers between devices with their start and end apart: 2, of which 2 were waited for; matrix products, arithmetic and copies ran while one was open for 0% of the time, Pallas kernels for 8%

profile of v2, /device:TPU:1, one launch (start us, length us, event | category | flops | bytes accessed | tf_op | source)
XLA Modules:
  0.0 46.6 jit_solution(3387257346286208660)
XLA Ops:
  0.6 5.1 %shard_map.122 = (f32[384,128]{1,0:T(8,128)}, s32[32,128]{1,0:T(8,128)}, s32[32,128]{1,0:T(8,128)}, s32[16,128]{1,0:T(8,128)}, s32[16,128]{1,0:T(8,128)}) custom-call(s32[1,32]{1,0:T(1,128)} %count_ref.1, s32[32,128]{1,0:T(8,128)} %bitcast.21, s32[32,128]{1,0:T(8,128)} %bitcast.22, s32[16,128]{1,0:T(8,128)} %bitcast.23, s32[16,128]{1,0:T(8,128)} %bitcast.24, ...), custom_call_target="tpu_custom_call" | custom-call | flops 1000000000 | bytes 10000000 | tf_op jit(solution)/shard_map/pallas_call | solution.py:193
  5.7 0.0 copy-start
  5.7 0.0 copy-start.1
  5.7 0.0 copy-start.2
  5.7 11.5 %all-to-all-start = ((f32[128,1,384]{2,1,0:T(1,128)}), f32[128,1,384]{2,1,0:T(1,128)S(1)}, u32[]{:S(2)}, u32[]{:S(2)}) async-start(f32[128,1,384]{2,1,0:T(1,128)} %bitcast.20), calls=%async_computation | async-start | bytes 393216 | tf_op jit(solution)/shard_map/all_to_all | solution.py:512
  17.2 0.0 copy-done
  17.2 0.0 copy-done.1
  17.3 0.0 copy-done.2
  17.3 1.2 %shard_map.123 = (f32[32,2048]{1,0:T(8,128)S(1)}, s32[32,128]{1,0:T(8,128)S(1)}) custom-call(f32[27,2048]{1,0:T(8,128)S(1)} %copy-done, f32[1,2048]{1,0:T(1,128)S(1)} %bitcast.14, s32[16,128]{1,0:T(8,128)S(1)} %bitcast.15), custom_call_target="tpu_custom_call" | custom-call | flops 1000000000 | bytes 10000000 | tf_op jit(solution)/shard_map/pallas_call | solution.py:264
  18.5 9.1 %all-to-all-done = f32[128,1,384]{2,1,0:T(1,128)S(1)} async-done(((f32[128,1,384]{2,1,0:T(1,128)}), f32[128,1,384]{2,1,0:T(1,128)S(1)}, u32[]{:S(2)}, u32[]{:S(2)}) %all-to-all-start) | async-done | bytes 196640 | tf_op jit(solution)/shard_map/all_to_all | solution.py:512
  27.6 2.3 %shard_map.124 = (f32[384,128]{1,0:T(8,128)}, f32[192,128]{1,0:T(8,128)S(1)}, f32[384,128]{1,0:T(8,128)S(1)}, s32[96,128]{1,0:T(8,128)S(1)}) custom-call(f32[384,128]{1,0:T(8,128)S(1)} %bitcast.13, f32[32,2048]{1,0:T(8,128)S(1)} %get-tuple-element.14.table_ref), custom_call_target="tpu_custom_call" | custom-call | flops 1000000000 | bytes 10000000 | tf_op jit(solution)/shard_map/pallas_call | solution.py:365
  29.9 4.4 %all-to-all-start.1 = ((f32[128,1,384]{2,1,0:T(1,128)}), f32[128,1,384]{2,1,0:T(1,128)S(1)}, u32[]{:S(2)}, u32[]{:S(2)}) async-start(f32[128,1,384]{2,1,0:T(1,128)} %bitcast.10), calls=%async_computation.1 | async-start | bytes 393216 | tf_op jit(solution)/shard_map/all_to_all | solution.py:512
  34.4 0.0 copy-start.4
  34.4 0.0 copy-start.5
  34.4 0.0 copy-start.6
  34.4 0.0 copy-start.7
  34.4 0.0 copy-start.8
  34.4 2.6 %shard_map.125.part_ref = f32[32,2048]{1,0:T(8,128)S(1)} custom-call(f32[192,128]{1,0:T(8,128)S(1)} %get-tuple-element.20.uv_ref, f32[384,128]{1,0:T(8,128)S(1)} %get-tuple-element.21.force_ref, s32[96,128]{1,0:T(8,128)S(1)} %get-tuple-element.22.index_ref, s32[32,128]{1,0:T(8,128)S(1)} %get-tuple-element.23.inv_ref), custom_call_target="tpu_custom_call" | custom-call | flops 1000000000 | bytes 10000000 | tf_op jit(solution)/shard_map/pallas_call | solution.py:432
  37.1 0.0 copy-start.3
  37.1 7.7 %all-to-all-done.1 = f32[128,1,384]{2,1,0:T(1,128)S(1)} async-done(((f32[128,1,384]{2,1,0:T(1,128)}), f32[128,1,384]{2,1,0:T(1,128)S(1)}, u32[]{:S(2)}, u32[]{:S(2)}) %all-to-all-start.1) | async-done | bytes 196640 | tf_op jit(solution)/shard_map/all_to_all | solution.py:512
  44.7 0.0 copy-done.4
  44.7 0.0 copy-done.5
  44.7 0.0 copy-done.6
  44.7 0.0 copy-done.7
  44.8 0.0 copy-done.8
  44.8 0.0 copy-done.3
  44.8 1.9 %shard_map.126 = (f32[3,4096]{1,0:T(4,128)}, f32[27,2048]{1,0:T(8,128)}) custom-call(f32[384,128]{1,0:T(8,128)S(1)} %bitcast.12, s32[32,128]{1,0:T(8,128)S(1)} %copy-done.5, s32[32,128]{1,0:T(8,128)S(1)} %copy-done.6, s32[16,128]{1,0:T(8,128)S(1)} %copy-done.7, s32[16,128]{1,0:T(8,128)S(1)} %copy-done.8, s32[16,128]{1,0:T(8,128)S(1)} %bitcast.17, ...), custom_call_target="tpu_custom_call" | custom-call | flops 1000000000 | bytes 10000000 | tf_op jit(solution)/shard_map/pallas_call | solution.py:496
Async XLA Ops:
  5.7 11.5 %copy-start = (f32[27,2048]{1,0:T(8,128)S(1)}, f32[27,2048]{1,0:T(8,128)}, u32[]{:S(2)}) copy-start(f32[27,2048]{1,0:T(8,128)} %coords_ref.1) | copy-start | bytes 663556
  5.7 11.5 %copy-start.1 = (f32[2048]{0:T(1024)S(1)}, f32[2048]{0:T(1024)}, u32[]{:S(2)}) copy-start(f32[2048]{0:T(1024)} %param.12) | copy-start | bytes 24580
  5.7 11.5 %copy-start.2 = (s32[1,2048]{1,0:T(1,128)S(1)}, s32[1,2048]{1,0:T(1,128)}, u32[]{:S(2)}) copy-start(s32[1,2048]{1,0:T(1,128)} %param.13) | copy-start | bytes 24580
  5.7 21.9 %all-to-all-start = ((f32[128,1,384]{2,1,0:T(1,128)}), f32[128,1,384]{2,1,0:T(1,128)S(1)}, u32[]{:S(2)}, u32[]{:S(2)}) async-start(f32[128,1,384]{2,1,0:T(1,128)} %bitcast.20), calls=%async_computation | async-start | bytes 393216 | tf_op jit(solution)/shard_map/all_to_all | solution.py:512
  29.9 14.8 %all-to-all-start.1 = ((f32[128,1,384]{2,1,0:T(1,128)}), f32[128,1,384]{2,1,0:T(1,128)S(1)}, u32[]{:S(2)}, u32[]{:S(2)}) async-start(f32[128,1,384]{2,1,0:T(1,128)} %bitcast.10), calls=%async_computation.1 | async-start | bytes 393216 | tf_op jit(solution)/shard_map/all_to_all | solution.py:512
  34.4 10.4 %copy-start.4 = (s32[2048]{0:T(1024)S(1)}, s32[2048]{0:T(1024)}, u32[]{:S(2)}) copy-start(s32[2048]{0:T(1024)} %param.19) | copy-start | bytes 24580
  34.4 10.4 %copy-start.5 = (s32[32,128]{1,0:T(8,128)S(1)}, s32[32,128]{1,0:T(8,128)}, u32[]{:S(2)}) copy-start(s32[32,128]{1,0:T(8,128)} %get-tuple-element.16.speer_ref) | copy-start | bytes 49156
  34.4 10.4 %copy-start.6 = (s32[32,128]{1,0:T(8,128)S(1)}, s32[32,128]{1,0:T(8,128)}, u32[]{:S(2)}) copy-start(s32[32,128]{1,0:T(8,128)} %get-tuple-element.17.sk_ref) | copy-start | bytes 49156
  34.4 10.4 %copy-start.7 = (s32[16,128]{1,0:T(8,128)S(1)}, s32[16,128]{1,0:T(8,128)}, u32[]{:S(2)}) copy-start(s32[16,128]{1,0:T(8,128)} %get-tuple-element.18.mpeer_ref) | copy-start | bytes 24580
  34.4 10.4 %copy-start.8 = (s32[16,128]{1,0:T(8,128)S(1)}, s32[16,128]{1,0:T(8,128)}, u32[]{:S(2)}) copy-start(s32[16,128]{1,0:T(8,128)} %get-tuple-element.19.mk_ref) | copy-start | bytes 24580
  37.1 7.7 %copy-start.3 = (s32[2048]{0:T(1024)S(1)}, s32[2048]{0:T(1024)}, u32[]{:S(2)}) copy-start(s32[2048]{0:T(1024)} %param.18) | copy-start | bytes 24580

commit v3 on v2

--- a/solution.py
+++ b/solution.py
@@ -67,20 +67,15 @@
 
 
 VM = pl.BlockSpec(memory_space=pltpu.VMEM)
-SM = pl.BlockSpec(memory_space=pltpu.SMEM)
 HB = pl.BlockSpec(memory_space=pltpu.HBM)
 
 
-def pack_body(
-    count_ref, *refs,
-):
-    sources, refs = refs[:8], refs[8:]
-    send_ref, speer_ref, sk_ref, mpeer_ref, mk_ref = refs[:5]
-    buffers, refs = refs[5:13], refs[13:]
-    sdest_ref, sslot_ref, mdest_ref, mslot_ref, mface_ref, mnode_ref, coords_ref, spos_ref = buffers
+def pack_body(*refs):
+    sources, send_ref, keys_ref, buffers, refs = refs[:9], refs[9], refs[10], refs[11:20], refs[20:]
+    coords_ref, spos_ref, sdest_ref, sslot_ref, mdest_ref, mslot_ref, mface_ref, mnode_ref, count_ref = buffers
     e_ref, b_ref, val_ref, turn_ref, cols_ref, cnt_ref, rows_ref, sems = refs
     copies = [
-        pltpu.make_async_copy(sources[i], buffers[i], sems.at[i]) for i in range(8)
+        pltpu.make_async_copy(sources[i], buffers[i], sems.at[i]) for i in range(9)
     ]
     for copy in copies:
         copy.start()
@@ -92,15 +87,12 @@
         return owner, dest & (NBIN - 1), (slot & 255) + 1
 
     half = LANES // 2
-    for first, rows, dest_ref, slot_ref, peer_ref in (
-        (0, SB, sdest_ref, sslot_ref, speer_ref),
-        (SB, MB, mdest_ref, mslot_ref, mpeer_ref),
-    ):
+    for first, rows, dest_ref, slot_ref in ((0, SB, sdest_ref, sslot_ref), (SB, MB, mdest_ref, mslot_ref)):
         owner, col, code = keys(dest_ref[...], slot_ref[...])
         e_ref[first:first + rows] = owner
         b_ref[first:first + rows] = col
         val_ref[6, first:first + rows] = code.astype(F32)
-        peer_ref[...] = owner
+        keys_ref[first:first + rows] = owner
         cell = (owner * NBIN + col).astype(F32)
         turn_ref[first:first + rows] = cell
         turn_ref[half + first:half + first + rows] = pltpu.roll(cell, half, axis=1)
@@ -147,7 +139,7 @@
         high = x.astype(BF16).astype(F32)
         return high if i < 3 else x - high
 
-    def slots(first, last, cap, rows, kout):
+    def slots(first, last, cap, rows):
         seen = jnp.zeros((NBIN, LANES), F32)
         total = jnp.zeros((7 * rows, LANES), F32)
         zero = jnp.zeros((rows, LANES), BF16)
@@ -169,7 +161,7 @@
                 k = b_ref[r:r + 1, :] * cap + rank.astype(I32)
                 if first == 0:
                     k = jnp.where(lane_row < count_ref[0, i], k, -1)
-                kout[i:i + 1, :] = k
+                keys_ref[SB + MB + r:SB + MB + r + 1, :] = k
                 mine = slot_rows(rows) == wide16(k, rows)
                 parts = []
                 for j in (0, 1, 2, 6, 3, 4, 5):
@@ -181,25 +173,23 @@
             total = total + dot_nt(jnp.concatenate(left, 1), jnp.concatenate(right, 1))
         return jnp.concatenate([total[0:3 * rows] + total[4 * rows:], total[3 * rows:4 * rows]], 0)
 
-    rows_ref[0:4 * SK] = slots(0, SB, 8, SK, sk_ref)
-    rows_ref[4 * SK:] = slots(SB, SB + MB, 4, MK, mk_ref)
+    rows_ref[0:4 * SK] = slots(0, SB, 8, SK)
+    rows_ref[4 * SK:] = slots(SB, SB + MB, 4, MK)
     for i in range(3):
         send_ref[pl.ds(i, DEV, stride=3), :] = rows_ref[i * LANES:(i + 1) * LANES].T
 
 
 def pack(count, sdest, sslot, spos, mdest, mslot, mface, mnode, coords):
     blocks = SB + MB
-    arrays = (sdest, sslot, mdest, mslot, mface, mnode, coords, spos)
+    arrays = (coords, spos, sdest, sslot, mdest, mslot, mface, mnode)
     return call(
         pack_body,
         (
             jax.ShapeDtypeStruct((3 * DEV, LANES), F32),
-            jax.ShapeDtypeStruct((SB, LANES), I32),
-            jax.ShapeDtypeStruct((SB, LANES), I32),
-            jax.ShapeDtypeStruct((MB, LANES), I32),
-            jax.ShapeDtypeStruct((MB, LANES), I32),
+            jax.ShapeDtypeStruct((2 * blocks, LANES), I32),
         ),
         [pltpu.VMEM(x.shape, x.dtype) for x in arrays] + [
+            pltpu.SMEM(count.shape, I32),
             pltpu.VMEM((blocks, LANES), I32),
             pltpu.VMEM((blocks, LANES), I32),
             pltpu.VMEM((7, blocks, LANES), F32),
@@ -207,12 +197,12 @@
             pltpu.VMEM((LANES, LANES), F32),
             pltpu.VMEM((blocks, 16, LANES), F32),
             pltpu.VMEM((3 * LANES, LANES), F32),
-            pltpu.SemaphoreType.DMA((8,)),
+            pltpu.SemaphoreType.DMA((9,)),
         ],
-        in_specs=[SM] + [HB] * 8,
+        in_specs=[HB] * 9,
         cost=10**9,
         vmem=60 * 1024 * 1024,
-    )(count, *arrays)
+    )(*arrays, count)
 
 
 def quadratic(low, mid, high):
@@ -441,13 +431,15 @@
 
 
 def finish_body(
-    back_ref, speer_ref, sk_ref, mpeer_ref, mk_ref, mface_ref, mnode_ref, part_ref,
+    back_ref, keys_ref, mface_ref, mnode_ref, part_ref,
     slave_ref, face_ref, rows_ref, own_ref,
 ):
     for i in range(3):
         rows_ref[i * LANES:(i + 1) * LANES] = back_ref[pl.ds(i, DEV, stride=3), :].T
 
-    def collect(peer, slot, base, slots):
+    def collect(block, base, slots):
+        peer = keys_ref[block:block + 8]
+        slot = keys_ref[SB + MB + block:SB + MB + block + 8]
         at_slot = [slot == k for k in range(slots)]
         for c in range(3):
             out = jnp.zeros((8, LANES), F32)
@@ -457,7 +449,7 @@
             yield c, out
 
     for m in range(MB // 8):
-        for c, out in collect(mpeer_ref[8 * m:8 * m + 8], mk_ref[8 * m:8 * m + 8], 3 * SK, MK):
+        for c, out in collect(SB + 8 * m, 3 * SK, MK):
             own_ref[c, 8 * m:8 * m + 8] = out
 
     sub = iota((32, LANES), 0)
@@ -486,13 +478,13 @@
         face_ref[:, at] = (part_ref[:, at] + share)[0:27]
 
     for m in range(SB // 8):
-        for c, out in collect(speer_ref[8 * m:8 * m + 8], sk_ref[8 * m:8 * m + 8], 0, SK):
+        for c, out in collect(8 * m, 0, SK):
             for r in range(8):
                 at = (8 * m + r) * LANES
                 slave_ref[c:c + 1, at:at + LANES] = out[r:r + 1, :]
 
 
-def finish(back, speer, sk, mpeer, mk, mface, mnode, part):
+def finish(back, keys, mface, mnode, part):
     return call(
         finish_body,
         (
@@ -504,7 +496,7 @@
             pltpu.VMEM((3, MB, LANES), F32),
         ],
         cost=10**9,
-    )(back, speer, sk, mpeer, mk, mface, mnode, part)
+    )(back, keys, mface, mnode, part)
 
 
 def exchange(x):
@@ -519,7 +511,7 @@
 ):
     mface = mirror_face.reshape(MB, LANES)
     mnode = mirror_node.reshape(MB, LANES)
-    send, speer, sk, mpeer, mk = pack(
+    send, keys = pack(
         block_count,
         slave_dest.reshape(SB, LANES),
         face_slot.reshape(SB, LANES),
@@ -537,7 +529,7 @@
     back, uv, force, index = forces(recv, table)
     returned = exchange(back)
     part = react(uv, force, index, inv)
-    return finish(returned, speer, sk, mpeer, mk, mface, mnode, part)
+    return finish(returned, keys, mface, mnode, part)
 
 
 def solution(mesh):

time: 46.9 us -> 46.1 us (0.983)
  Pallas kernels: 13.1 us -> 12.4 us
    pallas_call x1, Pallas kernels: 5.06 us -> 4.33 us  [pack(): call(pack_body, (jax.ShapeDtypeStruct((3 * DEV, LANES), F32), jax.ShapeDt...]
where the time goes in v3:
time: 46.1 us; the launch traced here: 45.9 us
  waiting for transfers between devices  16.8 us (36%)
  starting transfers between devices  15.9 us (34%)
  Pallas kernels  12.4 us (27%)
  between operations  0.74 us (2%)
    all_to_all x2, waiting for transfers between devices, exchange(): lax.all_to_all(x, ('mech', 'bin'), split_axis=0, concat_axis=0, tiled=True)  16.8 us
    all_to_all x2, starting transfers between devices, exchange(): lax.all_to_all(x, ('mech', 'bin'), split_axis=0, concat_axis=0, tiled=True)  15.9 us
    pallas_call x1, Pallas kernels, pack(): call(pack_body, (jax.ShapeDtypeStruct((3 * DEV, LANES), F32), jax.ShapeDt...  4.33 us
    pallas_call x1, Pallas kernels, react(): call(react_body, jax.ShapeDtypeStruct((32, FT * LANES), F32), [pltpu.VMEM...  2.64 us
    pallas_call x1, Pallas kernels, forces(): call(force_body, (jax.ShapeDtypeStruct((3 * DEV, LANES), F32), jax.ShapeD...  2.28 us
    pallas_call x1, Pallas kernels, finish(): call(finish_body, (jax.ShapeDtypeStruct((3, SB * LANES), F32), jax.ShapeD...  1.87 us
    pallas_call x1, Pallas kernels, order_faces(): call(order_body, (jax.ShapeDtypeStruct((32, faces), F32), jax.ShapeDtypeS...  1.24 us
  transfers between devices with their start and end apart: 2, of which 2 were waited for; matrix products, arithmetic and copies ran while one was open for 0% of the time, Pallas kernels for 8%

profile of v3, /device:TPU:1, one launch (start us, length us, event | category | flops | bytes accessed | tf_op | source)
XLA Modules:
  0.0 45.9 jit_solution(12706755095003460095)
XLA Ops:
  0.6 4.3 %shard_map.122 = (f32[384,128]{1,0:T(8,128)}, s32[96,128]{1,0:T(8,128)}) custom-call(f32[27,2048]{1,0:T(8,128)} %coords_ref.1, f32[3,4096]{1,0:T(4,128)} %refs_1_.1, s32[32,128]{1,0:T(8,128)} %bitcast.21, s32[32,128]{1,0:T(8,128)} %bitcast.22, s32[16,128]{1,0:T(8,128)} %bitcast.23, s32[16,128]{1,0:T(8,128)} %bitcast.24, s32[16,128]{1,0:T(8,128)} %bitcast.16, ...), custom_call_target="tpu_custom_call" | custom-call | flops 1000000000 | bytes 10000000 | tf_op jit(solution)/shard_map/pallas_call | solution.py:185
  5.0 0.0 copy-start
  5.0 0.0 copy-start.1
  5.0 0.0 copy-start.2
  5.0 11.5 %all-to-all-start = ((f32[128,1,384]{2,1,0:T(1,128)}), f32[128,1,384]{2,1,0:T(1,128)S(1)}, u32[]{:S(2)}, u32[]{:S(2)}) async-start(f32[128,1,384]{2,1,0:T(1,128)} %bitcast.20), calls=%async_computation | async-start | bytes 393216 | tf_op jit(solution)/shard_map/all_to_all | solution.py:504
  16.5 0.0 copy-done
  16.5 0.0 copy-done.1
  16.5 0.0 copy-done.2
  16.5 1.2 %shard_map.123 = (f32[32,2048]{1,0:T(8,128)S(1)}, s32[32,128]{1,0:T(8,128)S(1)}) custom-call(f32[27,2048]{1,0:T(8,128)S(1)} %copy-done, f32[1,2048]{1,0:T(1,128)S(1)} %bitcast.14, s32[16,128]{1,0:T(8,128)S(1)} %bitcast.15), custom_call_target="tpu_custom_call" | custom-call | flops 1000000000 | bytes 10000000 | tf_op jit(solution)/shard_map/pallas_call | solution.py:254
  17.8 9.1 %all-to-all-done = f32[128,1,384]{2,1,0:T(1,128)S(1)} async-done(((f32[128,1,384]{2,1,0:T(1,128)}), f32[128,1,384]{2,1,0:T(1,128)S(1)}, u32[]{:S(2)}, u32[]{:S(2)}) %all-to-all-start) | async-done | bytes 196640 | tf_op jit(solution)/shard_map/all_to_all | solution.py:504
  26.9 2.3 %shard_map.124 = (f32[384,128]{1,0:T(8,128)}, f32[192,128]{1,0:T(8,128)S(1)}, f32[384,128]{1,0:T(8,128)S(1)}, s32[96,128]{1,0:T(8,128)S(1)}) custom-call(f32[384,128]{1,0:T(8,128)S(1)} %bitcast.13, f32[32,2048]{1,0:T(8,128)S(1)} %get-tuple-element.11.table_ref), custom_call_target="tpu_custom_call" | custom-call | flops 1000000000 | bytes 10000000 | tf_op jit(solution)/shard_map/pallas_call | solution.py:355
  29.2 4.4 %all-to-all-start.1 = ((f32[128,1,384]{2,1,0:T(1,128)}), f32[128,1,384]{2,1,0:T(1,128)S(1)}, u32[]{:S(2)}, u32[]{:S(2)}) async-start(f32[128,1,384]{2,1,0:T(1,128)} %bitcast.10), calls=%async_computation.1 | async-start | bytes 393216 | tf_op jit(solution)/shard_map/all_to_all | solution.py:504
  33.6 0.0 copy-start.3
  33.6 0.0 copy-start.4
  33.6 0.0 copy-start.5
  33.7 2.6 %shard_map.125.part_ref = f32[32,2048]{1,0:T(8,128)S(1)} custom-call(f32[192,128]{1,0:T(8,128)S(1)} %get-tuple-element.14.uv_ref, f32[384,128]{1,0:T(8,128)S(1)} %get-tuple-element.15.force_ref, s32[96,128]{1,0:T(8,128)S(1)} %get-tuple-element.16.index_ref, s32[32,128]{1,0:T(8,128)S(1)} %get-tuple-element.17.inv_ref), custom_call_target="tpu_custom_call" | custom-call | flops 1000000000 | bytes 10000000 | tf_op jit(solution)/shard_map/pallas_call | solution.py:422
  36.3 7.7 %all-to-all-done.1 = f32[128,1,384]{2,1,0:T(1,128)S(1)} async-done(((f32[128,1,384]{2,1,0:T(1,128)}), f32[128,1,384]{2,1,0:T(1,128)S(1)}, u32[]{:S(2)}, u32[]{:S(2)}) %all-to-all-start.1) | async-done | bytes 196640 | tf_op jit(solution)/shard_map/all_to_all | solution.py:504
  44.0 0.0 copy-done.3
  44.0 0.0 copy-done.4
  44.0 0.0 copy-done.5
  44.0 1.9 %shard_map.126 = (f32[3,4096]{1,0:T(4,128)}, f32[27,2048]{1,0:T(8,128)}) custom-call(f32[384,128]{1,0:T(8,128)S(1)} %bitcast.12, s32[96,128]{1,0:T(8,128)S(1)} %copy-done.5, s32[16,128]{1,0:T(8,128)S(1)} %bitcast.17, s32[16,128]{1,0:T(8,128)S(1)} %bitcast.19, f32[32,2048]{1,0:T(8,128)S(1)} %shard_map.125.part_ref), custom_call_target="tpu_custom_call" | custom-call | flops 1000000000 | bytes 10000000 | tf_op jit(solution)/shard_map/pallas_call | solution.py:488
Async XLA Ops:
  5.0 11.5 %copy-start = (f32[27,2048]{1,0:T(8,128)S(1)}, f32[27,2048]{1,0:T(8,128)}, u32[]{:S(2)}) copy-start(f32[27,2048]{1,0:T(8,128)} %coords_ref.1) | copy-start | bytes 663556
  5.0 11.5 %copy-start.1 = (f32[2048]{0:T(1024)S(1)}, f32[2048]{0:T(1024)}, u32[]{:S(2)}) copy-start(f32[2048]{0:T(1024)} %param.12) | copy-start | bytes 24580
  5.0 11.5 %copy-start.2 = (s32[1,2048]{1,0:T(1,128)S(1)}, s32[1,2048]{1,0:T(1,128)}, u32[]{:S(2)}) copy-start(s32[1,2048]{1,0:T(1,128)} %param.13) | copy-start | bytes 24580
  5.0 21.9 %all-to-all-start = ((f32[128,1,384]{2,1,0:T(1,128)}), f32[128,1,384]{2,1,0:T(1,128)S(1)}, u32[]{:S(2)}, u32[]{:S(2)}) async-start(f32[128,1,384]{2,1,0:T(1,128)} %bitcast.20), calls=%async_computation | async-start | bytes 393216 | tf_op jit(solution)/shard_map/all_to_all | solution.py:504
  29.2 14.8 %all-to-all-start.1 = ((f32[128,1,384]{2,1,0:T(1,128)}), f32[128,1,384]{2,1,0:T(1,128)S(1)}, u32[]{:S(2)}, u32[]{:S(2)}) async-start(f32[128,1,384]{2,1,0:T(1,128)} %bitcast.10), calls=%async_computation.1 | async-start | bytes 393216 | tf_op jit(solution)/shard_map/all_to_all | solution.py:504
  33.6 10.4 %copy-start.3 = (s32[2048]{0:T(1024)S(1)}, s32[2048]{0:T(1024)}, u32[]{:S(2)}) copy-start(s32[2048]{0:T(1024)} %param.18) | copy-start | bytes 24580
  33.6 10.4 %copy-start.4 = (s32[2048]{0:T(1024)S(1)}, s32[2048]{0:T(1024)}, u32[]{:S(2)}) copy-start(s32[2048]{0:T(1024)} %param.19) | copy-start | bytes 24580
  33.6 10.4 %copy-start.5 = (s32[96,128]{1,0:T(8,128)S(1)}, s32[96,128]{1,0:T(8,128)}, u32[]{:S(2)}) copy-start(s32[96,128]{1,0:T(8,128)} %get-tuple-element.13.keys_ref) | copy-start | bytes 147460

commit v4 on v3

--- a/solution.py
+++ b/solution.py
@@ -73,7 +73,7 @@
 def pack_body(*refs):
     sources, send_ref, keys_ref, buffers, refs = refs[:9], refs[9], refs[10], refs[11:20], refs[20:]
     coords_ref, spos_ref, sdest_ref, sslot_ref, mdest_ref, mslot_ref, mface_ref, mnode_ref, count_ref = buffers
-    e_ref, b_ref, val_ref, turn_ref, cols_ref, cnt_ref, rows_ref, sems = refs
+    e_ref, b_ref, val_ref, parts_ref, turn_ref, cols_ref, cnt_ref, rows_ref, sems = refs
     copies = [
         pltpu.make_async_copy(sources[i], buffers[i], sems.at[i]) for i in range(9)
     ]
@@ -132,16 +132,19 @@
             val_ref[c, SB + 8 * m:SB + 8 * m + 8] = high
             val_ref[3 + c, SB + 8 * m:SB + 8 * m + 8] = point - high
 
+    x = spos_ref[...]
+    high = x.astype(BF16).astype(F32)
+    parts_ref[0] = high
+    parts_ref[1] = x - high
+
     def value(i, r):
         if r >= SB or i == 6:
             return val_ref[i, r:r + 1, :]
-        x = spos_ref[i % 3:i % 3 + 1, r * LANES:(r + 1) * LANES]
-        high = x.astype(BF16).astype(F32)
-        return high if i < 3 else x - high
-
-    def slots(first, last, cap, rows):
+        return parts_ref[i // 3, i % 3:i % 3 + 1, r * LANES:(r + 1) * LANES]
+
+    def slots(first, last, cap, rows, base):
         seen = jnp.zeros((NBIN, LANES), F32)
-        total = jnp.zeros((7 * rows, LANES), F32)
+        total = jnp.zeros((7 * rows, 2 * LANES), F32)
         zero = jnp.zeros((rows, LANES), BF16)
         for group in range(first, last, 4):
             left, right = [], []
@@ -159,22 +162,33 @@
                     before = before + jnp.where(same, 1.0, 0.0)
                 rank = jnp.sum(before, 0, keepdims=True)
                 k = b_ref[r:r + 1, :] * cap + rank.astype(I32)
+                place = k & (rows - 1)
                 if first == 0:
-                    k = jnp.where(lane_row < count_ref[0, i], k, -1)
+                    live = lane_row < count_ref[0, i]
+                    k = jnp.where(live, k, -1)
+                    place = jnp.where(live, place, -1)
                 keys_ref[SB + MB + r:SB + MB + r + 1, :] = k
-                mine = slot_rows(rows) == wide16(k, rows)
+                mine = slot_rows(rows) == wide16(place, rows)
                 parts = []
                 for j in (0, 1, 2, 6, 3, 4, 5):
                     x = jnp.broadcast_to(value(j, r), (16, LANES)).astype(BF16)
-                    parts.append(jnp.where(mine, jnp.concatenate([x] * (rows // 16), 0), zero))
+                    x = jnp.concatenate([x] * (rows // 16), 0) if rows > 16 else x
+                    parts.append(jnp.where(mine, x, zero))
                 left.append(jnp.concatenate(parts, 0))
-                right.append(one_hot(LANES, e_ref[r:r + 1, :]))
+                right.append(one_hot(2 * LANES, e_ref[r:r + 1, :] + jnp.where(k >= rows, LANES, 0)))
                 seen = seen + cnt_ref[r, 0:8]
             total = total + dot_nt(jnp.concatenate(left, 1), jnp.concatenate(right, 1))
-        return jnp.concatenate([total[0:3 * rows] + total[4 * rows:], total[3 * rows:4 * rows]], 0)
-
-    rows_ref[0:4 * SK] = slots(0, SB, 8, SK)
-    rows_ref[4 * SK:] = slots(SB, SB + MB, 4, MK)
+        for c in range(4):
+            for h in range(2):
+                lanes = slice(h * LANES, (h + 1) * LANES)
+                out = total[c * rows:(c + 1) * rows, lanes]
+                if c < 3:
+                    out = out + total[(4 + c) * rows:(5 + c) * rows, lanes]
+                at = base + (2 * c + h) * rows
+                rows_ref[at:at + rows] = out
+
+    slots(0, SB, 8, SK // 2, 0)
+    slots(SB, SB + MB, 4, MK // 2, 4 * SK)
     for i in range(3):
         send_ref[pl.ds(i, DEV, stride=3), :] = rows_ref[i * LANES:(i + 1) * LANES].T
 
@@ -193,6 +207,7 @@
             pltpu.VMEM((blocks, LANES), I32),
             pltpu.VMEM((blocks, LANES), I32),
             pltpu.VMEM((7, blocks, LANES), F32),
+            pltpu.VMEM((2,) + spos.shape, F32),
             pltpu.VMEM((LANES, LANES), F32),
             pltpu.VMEM((LANES, LANES), F32),
             pltpu.VMEM((blocks, 16, LANES), F32),
@@ -263,17 +278,21 @@
 
 
 def project(point, coef, stiff):
+    def with_slope(t, low, mid, high):
+        top = high * t
+        both = mid + top
+        return low + t * both, both + top
+
     def surface(u, v):
-        u2 = u + u
-        v2 = v + v
         x, tu, tv = [], [], []
         for c in range(3):
             k = coef[c]
-            h = [k[0][q] + u * (k[1][q] + u * k[2][q]) for q in range(3)]
-            d = [k[1][q] + u2 * k[2][q] for q in range(3)]
-            x.append(h[0] + v * (h[1] + v * h[2]))
+            along = [with_slope(u, k[0][q], k[1][q], k[2][q]) for q in range(3)]
+            value, slope = with_slope(v, *[h for h, _ in along])
+            d = [slope_u for _, slope_u in along]
+            x.append(value)
             tu.append(d[0] + v * (d[1] + v * d[2]))
-            tv.append(h[1] + v2 * h[2])
+            tv.append(slope)
         return x, tu, tv
 
     def inner(a, b):

time: 46.1 us -> 45.9 us (level)
  no operation moved by 1% of the time
where the time goes in v4:
time: 45.9 us; the launch traced here: 45.7 us
  waiting for transfers between devices  16.8 us (37%)
  starting transfers between devices  15.9 us (35%)
  Pallas kernels  12.2 us (27%)
  between operations  0.74 us (2%)
    all_to_all x2, waiting for transfers between devices, exchange(): lax.all_to_all(x, ('mech', 'bin'), split_axis=0, concat_axis=0, tiled=True)  16.8 us
    all_to_all x2, starting transfers between devices, exchange(): lax.all_to_all(x, ('mech', 'bin'), split_axis=0, concat_axis=0, tiled=True)  15.9 us
    pallas_call x1, Pallas kernels, pack(): call(pack_body, (jax.ShapeDtypeStruct((3 * DEV, LANES), F32), jax.ShapeDt...  4.26 us
    pallas_call x1, Pallas kernels, react(): call(react_body, jax.ShapeDtypeStruct((32, FT * LANES), F32), [pltpu.VMEM...  2.64 us
    pallas_call x1, Pallas kernels, forces(): call(force_body, (jax.ShapeDtypeStruct((3 * DEV, LANES), F32), jax.ShapeD...  2.18 us
    pallas_call x1, Pallas kernels, finish(): call(finish_body, (jax.ShapeDtypeStruct((3, SB * LANES), F32), jax.ShapeD...  1.87 us
    pallas_call x1, Pallas kernels, order_faces(): call(order_body, (jax.ShapeDtypeStruct((32, faces), F32), jax.ShapeDtypeS...  1.24 us
  transfers between devices with their start and end apart: 2, of which 2 were waited for; matrix products, arithmetic and copies ran while one was open for 0% of the time, Pallas kernels for 8%

profile of v4, /device:TPU:1, one launch (start us, length us, event | category | flops | bytes accessed | tf_op | source)
XLA Modules:
  0.0 45.7 jit_solution(12972121928545085776)
XLA Ops:
  0.6 4.3 %shard_map.122 = (f32[384,128]{1,0:T(8,128)}, s32[96,128]{1,0:T(8,128)}) custom-call(f32[27,2048]{1,0:T(8,128)} %coords_ref.1, f32[3,4096]{1,0:T(4,128)} %refs_1_.1, s32[32,128]{1,0:T(8,128)} %bitcast.21, s32[32,128]{1,0:T(8,128)} %bitcast.22, s32[16,128]{1,0:T(8,128)} %bitcast.23, s32[16,128]{1,0:T(8,128)} %bitcast.24, s32[16,128]{1,0:T(8,128)} %bitcast.16, ...), custom_call_target="tpu_custom_call" | custom-call | flops 1000000000 | bytes 10000000 | tf_op jit(solution)/shard_map/pallas_call | solution.py:199
  4.9 0.0 copy-start
  4.9 0.0 copy-start.1
  4.9 0.0 copy-start.2
  4.9 11.5 %all-to-all-start = ((f32[128,1,384]{2,1,0:T(1,128)}), f32[128,1,384]{2,1,0:T(1,128)S(1)}, u32[]{:S(2)}, u32[]{:S(2)}) async-start(f32[128,1,384]{2,1,0:T(1,128)} %bitcast.20), calls=%async_computation | async-start | bytes 393216 | tf_op jit(solution)/shard_map/all_to_all | solution.py:523
  16.4 0.0 copy-done
  16.4 0.0 copy-done.1
  16.5 0.0 copy-done.2
  16.5 1.2 %shard_map.123 = (f32[32,2048]{1,0:T(8,128)S(1)}, s32[32,128]{1,0:T(8,128)S(1)}) custom-call(f32[27,2048]{1,0:T(8,128)S(1)} %copy-done, f32[1,2048]{1,0:T(1,128)S(1)} %bitcast.14, s32[16,128]{1,0:T(8,128)S(1)} %bitcast.15), custom_call_target="tpu_custom_call" | custom-call | flops 1000000000 | bytes 10000000 | tf_op jit(solution)/shard_map/pallas_call | solution.py:269
  17.7 9.1 %all-to-all-done = f32[128,1,384]{2,1,0:T(1,128)S(1)} async-done(((f32[128,1,384]{2,1,0:T(1,128)}), f32[128,1,384]{2,1,0:T(1,128)S(1)}, u32[]{:S(2)}, u32[]{:S(2)}) %all-to-all-start) | async-done | bytes 196640 | tf_op jit(solution)/shard_map/all_to_all | solution.py:523
  26.8 2.2 %shard_map.124 = (f32[384,128]{1,0:T(8,128)}, f32[192,128]{1,0:T(8,128)S(1)}, f32[384,128]{1,0:T(8,128)S(1)}, s32[96,128]{1,0:T(8,128)S(1)}) custom-call(f32[384,128]{1,0:T(8,128)S(1)} %bitcast.13, f32[32,2048]{1,0:T(8,128)S(1)} %get-tuple-element.11.table_ref), custom_call_target="tpu_custom_call" | custom-call | flops 1000000000 | bytes 10000000 | tf_op jit(solution)/shard_map/pallas_call | solution.py:374
  29.0 4.4 %all-to-all-start.1 = ((f32[128,1,384]{2,1,0:T(1,128)}), f32[128,1,384]{2,1,0:T(1,128)S(1)}, u32[]{:S(2)}, u32[]{:S(2)}) async-start(f32[128,1,384]{2,1,0:T(1,128)} %bitcast.10), calls=%async_computation.1 | async-start | bytes 393216 | tf_op jit(solution)/shard_map/all_to_all | solution.py:523
  33.4 0.0 copy-start.3
  33.5 0.0 copy-start.4
  33.5 0.0 copy-start.5
  33.5 2.6 %shard_map.125.part_ref = f32[32,2048]{1,0:T(8,128)S(1)} custom-call(f32[192,128]{1,0:T(8,128)S(1)} %get-tuple-element.14.uv_ref, f32[384,128]{1,0:T(8,128)S(1)} %get-tuple-element.15.force_ref, s32[96,128]{1,0:T(8,128)S(1)} %get-tuple-element.16.index_ref, s32[32,128]{1,0:T(8,128)S(1)} %get-tuple-element.17.inv_ref), custom_call_target="tpu_custom_call" | custom-call | flops 1000000000 | bytes 10000000 | tf_op jit(solution)/shard_map/pallas_call | solution.py:441
  36.1 7.7 %all-to-all-done.1 = f32[128,1,384]{2,1,0:T(1,128)S(1)} async-done(((f32[128,1,384]{2,1,0:T(1,128)}), f32[128,1,384]{2,1,0:T(1,128)S(1)}, u32[]{:S(2)}, u32[]{:S(2)}) %all-to-all-start.1) | async-done | bytes 196640 | tf_op jit(solution)/shard_map/all_to_all | solution.py:523
  43.8 0.0 copy-done.3
  43.8 0.0 copy-done.4
  43.8 0.0 copy-done.5
  43.8 1.9 %shard_map.126 = (f32[3,4096]{1,0:T(4,128)}, f32[27,2048]{1,0:T(8,128)}) custom-call(f32[384,128]{1,0:T(8,128)S(1)} %bitcast.12, s32[96,128]{1,0:T(8,128)S(1)} %copy-done.5, s32[16,128]{1,0:T(8,128)S(1)} %bitcast.17, s32[16,128]{1,0:T(8,128)S(1)} %bitcast.19, f32[32,2048]{1,0:T(8,128)S(1)} %shard_map.125.part_ref), custom_call_target="tpu_custom_call" | custom-call | flops 1000000000 | bytes 10000000 | tf_op jit(solution)/shard_map/pallas_call | solution.py:507
Async XLA Ops:
  4.9 11.5 %copy-start = (f32[27,2048]{1,0:T(8,128)S(1)}, f32[27,2048]{1,0:T(8,128)}, u32[]{:S(2)}) copy-start(f32[27,2048]{1,0:T(8,128)} %coords_ref.1) | copy-start | bytes 663556
  4.9 11.5 %copy-start.1 = (f32[2048]{0:T(1024)S(1)}, f32[2048]{0:T(1024)}, u32[]{:S(2)}) copy-start(f32[2048]{0:T(1024)} %param.12) | copy-start | bytes 24580
  4.9 11.5 %copy-start.2 = (s32[1,2048]{1,0:T(1,128)S(1)}, s32[1,2048]{1,0:T(1,128)}, u32[]{:S(2)}) copy-start(s32[1,2048]{1,0:T(1,128)} %param.13) | copy-start | bytes 24580
  4.9 21.9 %all-to-all-start = ((f32[128,1,384]{2,1,0:T(1,128)}), f32[128,1,384]{2,1,0:T(1,128)S(1)}, u32[]{:S(2)}, u32[]{:S(2)}) async-start(f32[128,1,384]{2,1,0:T(1,128)} %bitcast.20), calls=%async_computation | async-start | bytes 393216 | tf_op jit(solution)/shard_map/all_to_all | solution.py:523
  29.0 14.8 %all-to-all-start.1 = ((f32[128,1,384]{2,1,0:T(1,128)}), f32[128,1,384]{2,1,0:T(1,128)S(1)}, u32[]{:S(2)}, u32[]{:S(2)}) async-start(f32[128,1,384]{2,1,0:T(1,128)} %bitcast.10), calls=%async_computation.1 | async-start | bytes 393216 | tf_op jit(solution)/shard_map/all_to_all | solution.py:523
  33.4 10.4 %copy-start.3 = (s32[2048]{0:T(1024)S(1)}, s32[2048]{0:T(1024)}, u32[]{:S(2)}) copy-start(s32[2048]{0:T(1024)} %param.18) | copy-start | bytes 24580
  33.5 10.4 %copy-start.4 = (s32[2048]{0:T(1024)S(1)}, s32[2048]{0:T(1024)}, u32[]{:S(2)}) copy-start(s32[2048]{0:T(1024)} %param.19) | copy-start | bytes 24580
  33.5 10.4 %copy-start.5 = (s32[96,128]{1,0:T(8,128)S(1)}, s32[96,128]{1,0:T(8,128)}, u32[]{:S(2)}) copy-start(s32[96,128]{1,0:T(8,128)} %get-tuple-element.13.keys_ref) | copy-start | bytes 147460
